TPU v7x, 32 devices: a whole 2x2x4 slice. The times are simulated.
32 devices in a mesh: mode: 8 (over y, x, core), orb: 4 (over z).
Axes of the slice: x: 2, y: 2, z: 4, core: 2. Of those that a mesh axis runs over, the one named last changes fastest.
Arguments:
- correlators: float32 [512, 2, 256, 256], P('mode', None, 'orb'), may hold values from -6 to 6
- density: float32 [2, 256, 256], P(None, 'orb'), may hold values from -6 to 6
- bare_hamiltonian: float32 [2, 256, 256], P(None, 'orb'), may hold values from -0.375 to 0.375
- coupling: float32 [512], P('mode'), may hold values from -0.25 to 0.25
- propagator: float32 [512, 512], P('mode'), may hold values from -0.25 to 0.25
Outputs:
- correlators_out: float32 [512, 2, 256, 256], P('mode', None, 'orb')
- density_out: float32 [2, 256, 256], P(None, 'orb')
All inputs are finite; a program needn't handle non-finite values.
Results may differ from a plain program's by a relative error of at most 0.0001.
Values sent between devices are 32-bit elements; how exact they have to be, the bound alone decides.
No kernel may reach another device: no remote copies, remote signals or barrier semaphores. Data moves between devices by JAX's collectives and lax.ppermute only.
A program may use at most 128 MiB of HBM per device.

v0:
```python
import jax
import jax.numpy as jnp
from jax import lax
from jax.experimental import pallas as pl
from jax.experimental.pallas import tpu as pltpu
from jax.sharding import PartitionSpec as P

time_step = 0.1
field_weight = 0.0625
tile_rows, tile_cols = 8, 128
out_shares = (1, 3, 6, 6)


def contract(form, first, second):
    return jnp.einsum(form, first, second, precision=lax.Precision.HIGHEST)


def embed(matrix):
    real, imag = matrix[0], matrix[1]
    return jnp.concatenate(
        [jnp.concatenate([real, -imag], axis=1), jnp.concatenate([imag, real], axis=1)], axis=0
    )


def product(first, second):
    flat = second.reshape(-1, second.shape[-1])
    return contract("ij,jk->ik", embed(first), flat).reshape(second.shape)


def generator(hamil):
    return jnp.stack([time_step * hamil[1], -time_step * hamil[0]])


def apply_step(gen, matrix):
    return matrix + product(gen, matrix) - product(matrix, gen)


def split(values):
    high = lax.reduce_precision(values, exponent_bits=8, mantissa_bits=7)
    return high.astype(jnp.bfloat16), (values - high).astype(jnp.bfloat16)


def split_in_kernel(values):
    high = values.astype(jnp.bfloat16)
    return high, (values - high.astype(jnp.float32)).astype(jnp.bfloat16)


def dot(first, second):
    return jnp.dot(first, second, preferred_element_type=jnp.float32)


def densities(dens, bare, coupled, norm):
    gen0 = generator(bare + field_weight * dens)
    coupled1 = apply_step(gen0, coupled) + time_step * norm * dens
    dens1 = dens + time_step * coupled1
    gen1 = generator(bare + field_weight * dens1)
    coupled2 = apply_step(gen1, coupled1) + time_step * norm * dens1
    dens2 = dens1 + time_step * coupled2
    gen2 = generator(bare + field_weight * dens2)
    source = apply_step(gen2, time_step * (apply_step(gen1, dens) + dens1))
    return (gen0, gen1, gen2), dens2, source


def last_density(gens, dens2, source, coupled_mixed, norm, norm_mixed):
    value = coupled_mixed
    for gen in gens:
        value = apply_step(gen, value)
    return dens2 + time_step * (value + norm_mixed * source + time_step * norm * dens2)


def swap(array, axis, offset):
    return lax.ppermute(array, axis, [(i, i ^ offset) for i in range(lax.axis_size(axis))])


def gather_by_doubling(array, axis):
    place = lax.axis_index(axis)
    offset, done, current = lax.axis_size(axis) // 2, 0, array
    while offset:
        other = swap(current, axis, offset)
        upper = (place & offset) != 0
        current = jnp.stack(
            [jnp.where(upper, other, current), jnp.where(upper, current, other)], axis=done
        )
        done, offset = done + 1, offset // 2
    return current.reshape((-1,) + array.shape)


def exchange(pieces, axis):
    return [swap(piece, axis, k) if k else piece for k, piece in enumerate(pieces)]


def by_place(received, place):
    current, offset = jnp.stack(received), 1
    while offset < len(received):
        pairs = current.reshape((-1, 2, offset) + received[0].shape)
        turned = jnp.concatenate([pairs[:, 1:], pairs[:, :1]], axis=1)
        current = jnp.where((place & offset) != 0, turned, pairs)
        offset *= 2
    return current.reshape((len(received),) + received[0].shape)


def after(array, other):
    return lax.optimization_barrier((array, other))[0]


def pack_kernel(depth, b, h, place_ref, flat_ref, *refs):
    outs, (held_ref, into, back) = refs[:-3], refs[-3:]
    fetched, stored = [], []
    for k, out in enumerate(outs):
        row = pl.multiple_of((place_ref[0] ^ k) * depth + b * tile_rows, tile_rows)
        source = flat_ref.at[:, pl.ds(row, tile_rows), h * tile_cols : (h + 1) * tile_cols]
        fetched.append(pltpu.make_async_copy(source, held_ref.at[k], into.at[k]))
        stored.append(pltpu.make_async_copy(held_ref.at[k], out, back.at[k]))
        fetched[-1].start()
    for fetch, store in zip(fetched, stored):
        fetch.wait()
        store.start()
    for store in stored:
        store.wait()


def pack(place, flat, groups, depth, b, h):
    piece = jax.ShapeDtypeStruct((flat.shape[0], tile_rows, tile_cols), jnp.float32)
    return pl.pallas_call(
        lambda *refs: pack_kernel(depth, b, h, *refs),
        out_shape=(piece,) * groups,
        in_specs=[pl.BlockSpec(memory_space=pltpu.SMEM), pl.BlockSpec(memory_space=pl.ANY)],
        out_specs=(pl.BlockSpec(memory_space=pl.ANY),) * groups,
        scratch_shapes=[
            pltpu.VMEM((groups,) + piece.shape, jnp.float32),
            pltpu.SemaphoreType.DMA((groups,)),
            pltpu.SemaphoreType.DMA((groups,)),
        ],
        name="pack",
    )(place, flat)


def mix_kernel(place_ref, high_ref, low_ref, *refs):
    groups = len(refs) - 4
    pieces, (out_ref, sum_ref, xh_ref, xl_ref) = refs[:groups], refs[groups:]
    place = place_ref[0]
    count = pieces[0].shape[0] // tile_rows
    modes = groups * count
    for k, piece in enumerate(pieces):
        base = pl.multiple_of((place ^ k) * count, count)
        for q in range(tile_rows):
            high, low = split_in_kernel(piece[pl.ds(q, count, stride=tile_rows), :])
            xh_ref[pl.ds(base, count), q * tile_cols : (q + 1) * tile_cols] = high
            xl_ref[pl.ds(base, count), q * tile_cols : (q + 1) * tile_cols] = low
    xh, xl = xh_ref[...], xl_ref[...]
    mixed = dot(high_ref[...], xh) + dot(high_ref[...], xl) + dot(low_ref[...], xh)
    for q in range(tile_rows):
        part = mixed[:, q * tile_cols : (q + 1) * tile_cols]
        out_ref[pl.ds(q, modes, stride=tile_rows), :] = part[:modes]
        sum_ref[q : q + 1, :] = part[modes : modes + 1]


def mix(place, high, low, pieces):
    groups, length = len(pieces), pieces[0].shape[0]
    modes = groups * length // tile_rows
    return pl.pallas_call(
        mix_kernel,
        out_shape=(
            jax.ShapeDtypeStruct((groups * length, tile_cols), jnp.float32),
            jax.ShapeDtypeStruct((tile_rows, tile_cols), jnp.float32),
        ),
        in_specs=[pl.BlockSpec(memory_space=pltpu.SMEM)]
        + [pl.BlockSpec(memory_space=pltpu.VMEM)] * (2 + groups),
        out_specs=(
            pl.BlockSpec(memory_space=pltpu.VMEM),
            pl.BlockSpec(memory_space=pltpu.VMEM),
        ),
        scratch_shapes=[
            pltpu.VMEM((modes, tile_rows * tile_cols), jnp.bfloat16),
            pltpu.VMEM((modes, tile_rows * tile_cols), jnp.bfloat16),
        ],
        name="mix",
    )(place, high, low, *pieces)


def step_of(real, imag, left, right):
    order = real.shape[-1]
    rh, rl = split_in_kernel(real)
    ih, il = split_in_kernel(imag)
    before = dot(left, jnp.concatenate([rh, ih, rl, il, rh, ih], axis=0))
    behind = dot(jnp.concatenate([rh, ih, rl, il, rh, ih], axis=1), right)
    return (
        real + (before[:order] - behind[:, :order]),
        imag + (before[order:] - behind[:, order:]),
    )


def steps_kernel(groups, rings, blocks, place_ref, scale_ref, left_ref, right_ref, source_ref, dens_ref, *refs):
    pieces, outs = refs[: len(blocks)], refs[len(blocks) : -4]
    g_ref, left_held, right_held, sem = refs[-4:]
    order = g_ref.shape[-1]
    rows = order // rings
    half = groups // 2
    deep = 1 + max(b for b, _ in blocks)
    turns = left_ref.shape[0]
    m = pl.program_id(0)

    def fetch(turn):
        return (
            pltpu.make_async_copy(left_ref.at[turn], left_held.at[turn], sem.at[turn, 0]),
            pltpu.make_async_copy(right_ref.at[turn], right_held.at[turn], sem.at[turn, 1]),
        )

    @pl.when(m == 0)
    def _():
        for turn in range(turns):
            for copy in fetch(turn):
                copy.start()

    for piece, (b, h) in zip(pieces, blocks):
        for c in range(2):
            for d in range(half):
                for z in range(rings):
                    row = z * rows + (d * deep + b) * tile_rows
                    g_ref[c, row : row + tile_rows, h * tile_cols : (h + 1) * tile_cols] = piece[
                        (c * half + d) * rings + z
                    ]

    def turn_step(turn, _):
        @pl.when(m == 0)
        def _():
            for copy in fetch(turn):
                copy.wait()

        real, imag = step_of(g_ref[0], g_ref[1], left_held[turn], right_held[turn])
        g_ref[0] = real
        g_ref[1] = imag
        return 0

    lax.fori_loop(0, turns, turn_step, 0)
    mixed, own = scale_ref[0, m], scale_ref[1, m]
    g_ref[...] = g_ref[...] + mixed * source_ref[...] + own * dens_ref[...]
    place = place_ref[0]
    for k, out in enumerate(outs):
        base = pl.multiple_of((place ^ k) * rows, rows)
        out[0] = g_ref[:, pl.ds(base, rows), :]


def steps(place, scales, left, right, source, dens, pieces, blocks, groups, rings, first, count):
    order = dens.shape[-1]
    rows = order // rings
    whole = pl.BlockSpec(memory_space=pltpu.VMEM)
    table = pl.BlockSpec(memory_space=pltpu.SMEM)
    apart = pl.BlockSpec(memory_space=pl.ANY)
    return pl.pallas_call(
        lambda *refs: steps_kernel(groups, rings, blocks, *refs),
        grid=(count,),
        out_shape=tuple(
            jax.ShapeDtypeStruct((count, 2, rows, order), jnp.float32) for _ in range(rings)
        ),
        in_specs=[table, table, apart, apart, whole, whole]
        + [
            pl.BlockSpec((groups * rings, tile_rows, tile_cols), lambda m: (0, first + m, 0))
            for _ in pieces
        ],
        out_specs=tuple(
            pl.BlockSpec((1, 2, rows, order), lambda m: (m, 0, 0, 0)) for _ in range(rings)
        ),
        scratch_shapes=[
            pltpu.VMEM((2, order, order), jnp.float32),
            pltpu.VMEM(left.shape, left.dtype),
            pltpu.VMEM(right.shape, right.dtype),
            pltpu.SemaphoreType.DMA((left.shape[0], 2)),
        ],
        name="steps",
    )(place, scales, left, right, source, dens, *pieces)


def densities_kernel(norm_ref, both_ref, coupled_ref, left_ref, right_ref, source_ref, dens_ref, held_ref):
    held_ref[0] = coupled_ref[...]
    held_ref[1] = both_ref[0]
    dens_ref[...] = both_ref[0]

    def turn_step(turn, _):
        real = time_step * (both_ref[1, 1] + field_weight * dens_ref[1])
        imag = -time_step * (both_ref[1, 0] + field_weight * dens_ref[0])
        rh, rl = split_in_kernel(real)
        ih, il = split_in_kernel(imag)
        upper = [rh, -ih, rh, -ih, rl, -il]
        lower = [ih, rh, ih, rh, il, rl]
        left_ref[turn] = jnp.concatenate(
            [jnp.concatenate(upper, axis=1), jnp.concatenate(lower, axis=1)], axis=0
        )
        first_columns = [rh, -ih, rh, -ih, rl, -il]
        last_columns = [ih, rh, ih, rh, il, rl]
        right_ref[turn] = jnp.concatenate(
            [jnp.concatenate(first_columns, axis=0), jnp.concatenate(last_columns, axis=0)], axis=1
        )
        first, second = turn == 0, turn == 1
        kept = jnp.where(first, 1.0, 0.0)
        scale = jnp.where(first, 0.0, jnp.where(second, time_step, 1.0))
        added = jnp.where(second, time_step, 0.0)

        def apply(which, _):
            real, imag = step_of(held_ref[which, 0], held_ref[which, 1], left_ref[turn], right_ref[turn])
            chain = which == 0
            keep = jnp.where(chain, 0.0, kept)
            take = jnp.where(chain, 1.0, scale)
            more = jnp.where(chain, time_step * norm_ref[0], added)
            held_ref[which, 0] = keep * held_ref[which, 0] + take * real + more * dens_ref[0]
            held_ref[which, 1] = keep * held_ref[which, 1] + take * imag + more * dens_ref[1]
            return 0

        lax.fori_loop(0, 2, apply, 0)
        grown = jnp.where(turn < 2, time_step, 0.0)
        dens_ref[...] = dens_ref[...] + grown * held_ref[0]
        return 0

    lax.fori_loop(0, 3, turn_step, 0)
    source_ref[...] = held_ref[1]


def tables(norm, both, coupled):
    order = coupled.shape[-1]
    whole = pl.BlockSpec(memory_space=pltpu.VMEM)
    matrix = jax.ShapeDtypeStruct((2, order, order), jnp.float32)
    return pl.pallas_call(
        densities_kernel,
        out_shape=(
            jax.ShapeDtypeStruct((3, 2 * order, 6 * order), jnp.bfloat16),
            jax.ShapeDtypeStruct((3, 6 * order, 2 * order), jnp.bfloat16),
            matrix,
            matrix,
        ),
        in_specs=[pl.BlockSpec(memory_space=pltpu.SMEM), whole, whole],
        out_specs=(whole,) * 4,
        scratch_shapes=[pltpu.VMEM((2, 2, order, order), jnp.float32)],
        name="densities",
    )(norm, both, coupled)


def on_device(correlators, density, bare_hamiltonian, coupling, propagator):
    local, _, rows, order = correlators.shape
    groups, rings = lax.axis_size("mode"), lax.axis_size("orb")
    place, ring = lax.axis_index("mode"), lax.axis_index("orb")
    modes = local * groups
    owned = local // rings
    depth = 2 * rows // groups

    flat = correlators.reshape(local, 2 * rows, order)
    deep, wide = depth // tile_rows, order // tile_cols
    blocks = [(b, h) for b in range(deep) for h in range(wide)]
    here = place.reshape(1)

    mine = jnp.concatenate(
        [propagator, jnp.zeros((tile_rows, modes), jnp.float32).at[0, :local].set(coupling)]
    )
    even = [swap(mine, "mode", k) if k else mine for k in range(0, groups, 2)]
    odd = swap(jnp.stack(even), "mode", 1)
    gathered = by_place(
        [part for j in range(groups // 2) for part in (even[j], odd[j])], place
    )
    weights = gathered[:, local, :local].reshape(modes)
    full = gathered[:, :local].reshape(modes, modes)
    mixed_weights = contract("m,mn->n", weights, full)
    norm = jnp.sum(weights * weights)
    norm_mixed = jnp.sum(mixed_weights * weights)
    rows16 = jnp.zeros((2 * tile_rows, modes), jnp.float32).at[0].set(mixed_weights)
    high, low = split(jnp.concatenate([full, rows16]))

    near = place & 1
    small = jnp.stack([density, bare_hamiltonian])
    small = lax.dynamic_slice_in_dim(small, near * (rows // 2), rows // 2, 2)
    small = exchange([small] * rings, "orb")

    share = rows // groups
    count = len(blocks)
    packed = [pack(here, flat, groups, depth, *blocks[0])]
    packed.append(pack(here, after(flat, packed[0][0]), groups, depth, *blocks[1]))
    wholes, sums, mixes = [], {}, []
    for turn, (b, h) in enumerate(blocks):
        pieces = exchange([piece.reshape(-1, tile_cols) for piece in packed[turn]], "mode")
        ready = after(here, wholes[turn - 2]) if turn > 1 else here
        mixed, sums[b, h] = mix(ready, high, low, pieces)
        mixes.append(mixed)
        mixed = mixed.reshape(groups * rings, owned * tile_rows, tile_cols)
        wholes.append(lax.all_to_all(mixed, ("mode", "orb"), 0, 0, tiled=True))
        if turn + 2 < count:
            ready = after(flat, wholes[turn - 1] if turn else mixes[0])
            packed.append(pack(here, ready, groups, depth, *blocks[turn + 2]))
        if turn == 0:
            reached = (mixes[0], packed[2][0])
            coupled = jnp.sum(coupling[:, None, None, None] * after(correlators, reached), axis=0)
            coupled = [
                lax.dynamic_slice_in_dim(coupled, (place ^ k) * share, share, 1)
                for k in range(groups)
            ]
            coupled = exchange(coupled, "mode")
        if turn == 1:
            reached = (wholes[0], packed[3][0])
            coupled = sum(after(tuple(coupled), reached))
            coupled = exchange([coupled] * rings, "orb")
            small = by_place(after(tuple(small), reached), ring)
            other = swap(small, "mode", 1)
        if turn == 2:
            coupled = by_place(after(tuple(coupled), wholes[1]), ring)
            coupled = exchange([coupled] * groups, "mode")
            other = after(other, wholes[1])
            both = jnp.stack(
                [jnp.where(near == 1, other, small), jnp.where(near == 1, small, other)], axis=3
            )
            both = jnp.moveaxis(both, 0, 2).reshape(2, 2, order, order)
        if turn == 3:
            coupled = by_place(after(tuple(coupled), wholes[2]), place)
    coupled = coupled.transpose(2, 1, 0, 3, 4).reshape(2, order, order)
    left, right, source, dens2 = tables(norm.reshape(1), both, coupled)
    own_coupling = lax.dynamic_slice_in_dim(coupling, ring * owned, owned, 0)
    own_rows = lax.dynamic_slice_in_dim(propagator, ring * owned, owned, 0)
    scales = jnp.stack([contract("mn,n->m", own_rows, weights), time_step * own_coupling])

    stacks = jnp.zeros(correlators.shape, jnp.float32)
    first, finished = 0, []
    for share in out_shares:
        chunk = share * owned // sum(out_shares)
        parts = steps(
            ring.reshape(1), scales[:, first : first + chunk], left, right, source, dens2,
            wholes, blocks, groups, rings, first, chunk,
        )
        finished.append(parts[0])
        for k, part in enumerate(parts):
            part = swap(part, "orb", k) if k else part
            stacks = lax.dynamic_update_slice(stacks, part, ((ring ^ k) * owned + first, 0, 0, 0))
        first += chunk

    summed = jnp.stack([sums[block] for block in blocks])
    summed = gather_by_doubling(after(summed, finished[0]), "orb")
    summed = gather_by_doubling(after(summed, finished[-1]), "mode")
    summed = summed.reshape((groups * rings,) + summed.shape[2:])
    scales = jnp.stack([norm_mixed, time_step * norm]).reshape(2, 1)
    parts = steps(
        ring.reshape(1), scales, left, right, source, dens2,
        [summed[:, k] for k in range(len(blocks))], blocks, groups, rings, 0, 1,
    )
    dens = lax.dynamic_slice_in_dim(dens2, ring * rows, rows, 1) + time_step * parts[0][0]
    return stacks, dens


def on_device_plain(correlators, density, bare_hamiltonian, coupling, propagator):
    local, _, rows, order = correlators.shape
    groups, rings = lax.axis_size("mode"), lax.axis_size("orb")
    ring = lax.axis_index("orb")
    owned = local // rings
    full = lax.all_gather(propagator, "mode", axis=0, tiled=True)
    weights = lax.all_gather(coupling, "mode", axis=0, tiled=True)
    mixed_weights = contract("m,mn->n", weights, full)
    norm, norm_mixed = jnp.sum(weights * weights), jnp.sum(mixed_weights * weights)
    both = lax.all_gather(jnp.stack([density, bare_hamiltonian]), "orb", axis=2, tiled=True)
    sums = jnp.stack(
        [
            contract("m,mcij->cij", coupling, correlators),
            contract(
                "m,mcij->cij",
                lax.dynamic_slice_in_dim(mixed_weights, lax.axis_index("mode") * local, local, 0),
                correlators,
            ),
        ]
    )
    sums = lax.all_gather(lax.psum(sums, "mode"), "orb", axis=2, tiled=True)
    gens, dens2, source = densities(both[0], both[1], sums[0], norm)
    entries = lax.all_to_all(correlators.reshape(local, groups, -1), "mode", 1, 0, tiled=True)
    mixed = contract("mn,nx->mx", full, entries.reshape(full.shape[0], -1))
    mixed = lax.all_to_all(mixed.reshape(groups * rings, -1), ("mode", "orb"), 0, 0, tiled=True)
    whole = mixed.reshape(groups, rings, owned, -1).transpose(2, 1, 0, 3)
    whole = whole.reshape(owned, rings, 2, rows, order).transpose(0, 2, 1, 3, 4)
    whole = whole.reshape(owned, 2, order, order)
    for gen in gens:
        whole = jax.vmap(lambda matrix, gen=gen: apply_step(gen, matrix))(whole)
    own_coupling = lax.dynamic_slice_in_dim(coupling, ring * owned, owned, 0)
    own_rows = lax.dynamic_slice_in_dim(propagator, ring * owned, owned, 0)
    scale = contract("mn,n->m", own_rows, weights)
    whole = (
        whole
        + scale[:, None, None, None] * source[None]
        + time_step * own_coupling[:, None, None, None] * dens2[None]
    )
    stacks = lax.all_to_all(whole, "orb", split_axis=2, concat_axis=0, tiled=True)
    dens = last_density(gens, dens2, source, sums[1], norm, norm_mixed)
    return stacks, lax.dynamic_slice_in_dim(dens, ring * rows, rows, 1)


def solution(mesh):
    in_specs = (
        P("mode", None, "orb", None),
        P(None, "orb", None),
        P(None, "orb", None),
        P("mode"),
        P("mode", None),
    )
    out_specs = (P("mode", None, "orb", None), P(None, "orb", None))
    groups, rings = mesh.shape["mode"], mesh.shape["orb"]

    def body(correlators, *others):
        local, _, rows, order = correlators.shape
        fits = (
            groups > 1
            and groups & (groups - 1) == 0
            and rings & (rings - 1) == 0
            and rows % (groups * tile_rows) == 0
            and order % tile_cols == 0
            and 2 * rows * order >= 4 * groups * tile_rows * tile_cols
            and local % (2 * tile_rows) == 0
            and local % (rings * sum(out_shares)) == 0
        )
        return (on_device if fits else on_device_plain)(correlators, *others)

    return jax.shard_map(
        body, mesh=mesh, in_specs=in_specs, out_specs=out_specs, check_vma=False
    )
```

profile of v0, /device:TPU:8, one launch (start us, length us, event | category | flops | bytes accessed | tf_op | source)
XLA Modules:
  0.0 585.4 jit_solution(9766191481934556464)
XLA Ops:
  5.1 2.9 collective-permute-done
  8.0 3.6 collective-permute-done.1
  21.8 13.1 %collective-permute-done.10.refs_4_ = f32[512,128]{1,0:T(8,128)S(1)} collective-permute-done((f32[512,128]{1,0:T(8,128)}, f32[512,128]{1,0:T(8,128)S(1)}, u32[]{:S(2)}, u32[]{:S(2)}) %collective-permute-start.10) | collective-permute-done | bytes 262176 | tf_op jit(solution)/shard_map/ppermute | solution.py:72
  36.1 3.3 collective-permute-done.11.refs_5_
  42.8 4.4 collective-permute-done.9.refs_3_
  48.0 5.6 mix.4
  53.6 5.4 all-to-all-start
  67.5 13.5 %collective-permute-done.16.refs_2_ = f32[512,128]{1,0:T(8,128)S(1)} collective-permute-done((f32[512,128]{1,0:T(8,128)}, f32[512,128]{1,0:T(8,128)S(1)}, u32[]{:S(2)}, u32[]{:S(2)}) %collective-permute-start.16) | collective-permute-done | bytes 262176 | tf_op jit(solution)/shard_map/ppermute | solution.py:72
  81.1 7.6 %collective-permute-done.17.refs_3_ = f32[512,128]{1,0:T(8,128)S(1)} collective-permute-done((f32[512,128]{1,0:T(8,128)}, f32[512,128]{1,0:T(8,128)S(1)}, u32[]{:S(2)}, u32[]{:S(2)}) %collective-permute-start.17) | collective-permute-done | bytes 262176 | tf_op jit(solution)/shard_map/ppermute | solution.py:72
  88.7 13.2 %collective-permute-done.20.refs_6_ = f32[512,128]{1,0:T(8,128)} collective-permute-done((f32[512,128]{1,0:T(8,128)}, f32[512,128]{1,0:T(8,128)}, u32[]{:S(2)}, u32[]{:S(2)}) %collective-permute-start.20) | collective-permute-done | bytes 262176 | tf_op jit(solution)/shard_map/ppermute | solution.py:72
  101.9 6.0 %collective-permute-done.21.refs_7_ = f32[512,128]{1,0:T(8,128)} collective-permute-done((f32[512,128]{1,0:T(8,128)}, f32[512,128]{1,0:T(8,128)}, u32[]{:S(2)}, u32[]{:S(2)}) %collective-permute-start.21) | collective-permute-done | bytes 262176 | tf_op jit(solution)/shard_map/ppermute | solution.py:72
  108.0 5.6 mix.5
  114.9 4.5 all-to-all-start.1
  127.8 13.5 %collective-permute-done.40.refs_2_ = f32[512,128]{1,0:T(8,128)S(1)} collective-permute-done((f32[512,128]{1,0:T(8,128)}, f32[512,128]{1,0:T(8,128)S(1)}, u32[]{:S(2)}, u32[]{:S(2)}) %collective-permute-start.40) | collective-permute-done | bytes 262176 | tf_op jit(solution)/shard_map/ppermute | solution.py:72
  141.5 7.5 %collective-permute-done.41.refs_3_ = f32[512,128]{1,0:T(8,128)S(1)} collective-permute-done((f32[512,128]{1,0:T(8,128)}, f32[512,128]{1,0:T(8,128)S(1)}, u32[]{:S(2)}, u32[]{:S(2)}) %collective-permute-start.41) | collective-permute-done | bytes 262176 | tf_op jit(solution)/shard_map/ppermute | solution.py:72
  149.1 13.0 %collective-permute-done.44.refs_6_ = f32[512,128]{1,0:T(8,128)S(1)} collective-permute-done((f32[512,128]{1,0:T(8,128)}, f32[512,128]{1,0:T(8,128)S(1)}, u32[]{:S(2)}, u32[]{:S(2)}) %collective-permute-start.44) | collective-permute-done | bytes 262176 | tf_op jit(solution)/shard_map/ppermute | solution.py:72
  162.2 6.0 %collective-permute-done.45.refs_7_ = f32[512,128]{1,0:T(8,128)S(1)} collective-permute-done((f32[512,128]{1,0:T(8,128)}, f32[512,128]{1,0:T(8,128)S(1)}, u32[]{:S(2)}, u32[]{:S(2)}) %collective-permute-start.45) | collective-permute-done | bytes 262176 | tf_op jit(solution)/shard_map/ppermute | solution.py:72
  168.9 5.6 mix.6
  174.5 4.4 all-to-all-start.2
  179.2 4.3 multiply_reduce_fusion
  197.4 4.2 collective-permute-start.5
  206.1 11.4 %collective-permute-done.4 = f32[2,2,32,256]{3,2,1,0:T(8,128)S(1)} collective-permute-done((f32[2,2,32,256]{3,2,1,0:T(8,128)S(1)}, f32[2,2,32,256]{3,2,1,0:T(8,128)S(1)}, u32[]{:S(2)}, u32[]{:S(2)}) %collective-permute-start.4) | collective-permute-done | bytes 131104 | tf_op jit(solution)/shard_map/ppermute | solution.py:72
  220.1 14.1 %collective-permute-done.5 = f32[2,2,32,256]{3,2,1,0:T(8,128)S(1)} collective-permute-done((f32[2,2,32,256]{3,2,1,0:T(8,128)S(1)}, f32[2,2,32,256]{3,2,1,0:T(8,128)S(1)}, u32[]{:S(2)}, u32[]{:S(2)}) %collective-permute-start.5) | collective-permute-done | bytes 131104 | tf_op jit(solution)/shard_map/ppermute | solution.py:72
  234.2 4.6 collective-permute-done.6
  243.8 4.4 collective-permute-done.47.refs_2_
  252.7 3.1 collective-permute-start.52
  256.0 10.9 %collective-permute-done.50.refs_5_ = f32[512,128]{1,0:T(8,128)S(1)} collective-permute-done((f32[512,128]{1,0:T(8,128)S(1)}, f32[512,128]{1,0:T(8,128)S(1)}, u32[]{:S(2)}, u32[]{:S(2)}) %collective-permute-start.50) | collective-permute-done | bytes 262176 | tf_op jit(solution)/shard_map/ppermute | solution.py:72
  270.0 5.6 mix.7
  276.9 3.2 all-to-all-start.3
  285.5 12.3 %collective-permute-done.36 = f32[4,2,8,256]{3,2,0,1:T(8,128)S(1)} collective-permute-done((f32[4,2,8,256]{3,2,0,1:T(8,128)S(1)}, f32[4,2,8,256]{3,2,0,1:T(8,128)S(1)}, u32[]{:S(2)}, u32[]{:S(2)}) %collective-permute-start.36) | collective-permute-done | bytes 65568 | tf_op jit(solution)/shard_map/ppermute | solution.py:72
  304.1 12.8 %densities.1 = (bf16[3,512,1536]{2,1,0:T(8,128)(2,1)}, bf16[3,1536,512]{2,1,0:T(8,128)(2,1)}, f32[2,256,256]{2,1,0:T(8,128)}, f32[2,256,256]{2,1,0:T(8,128)}) custom-call(f32[1]{0:T(128)} %bitcast.18.norm_ref, f32[2,2,256,256]{3,2,1,0:T(8,128)} %bitcast.231, f32[2,256,256]{2,1,0:T(8,128)} %bitcast.239), custom_call_target="tpu_custom_call" | custom-call | tf_op jit(solution)/shard_map/densities/pallas_call | solution.py:322
  316.9 12.0 %all-to-all-done.3.refs_9_ = f32[32,128,128]{2,1,0:T(8,128)} async-done(((f32[32,128,128]{2,1,0:T(8,128)}), f32[32,128,128]{2,1,0:T(8,128)}, u32[]{:S(2)}, u32[]{:S(2)}) %all-to-all-start.3) | async-done | bytes 2097184 | tf_op jit(solution)/shard_map/all_to_all | solution.py:382
  328.9 7.2 %steps.5 = (f32[1,2,64,256]{3,2,1,0:T(8,128)}, f32[1,2,64,256]{3,2,1,0:T(8,128)}, f32[1,2,64,256]{3,2,1,0:T(8,128)}, f32[1,2,64,256]{3,2,1,0:T(8,128)}) custom-call(s32[1]{0:T(128)} %bitcast.refs_0_, f32[2,1]{1,0:T(2,128)} %bitcast.274, bf16[3,512,1536]{2,1,0:T(8,128)(2,1)} %get-tuple-element.178.refs_2_, bf16[3,1536,512]{2,1,0:T(8,128)(2,1)} %get-tuple-element.179.refs_3_, ...), custom_call_target="tpu_custom_call" | custom-call | tf_op jit(solution)/shard_map/steps/pallas_call | solution.py:250
  337.6 3.1 collective-permute-done.65
  346.4 13.9 %steps.6 = (f32[3,2,64,256]{3,2,1,0:T(8,128)}, f32[3,2,64,256]{3,2,1,0:T(8,128)}, f32[3,2,64,256]{3,2,1,0:T(8,128)}, f32[3,2,64,256]{3,2,1,0:T(8,128)}) custom-call(s32[1]{0:T(128)} %bitcast.refs_0_, f32[2,3]{1,0:T(2,128)} %slice.159.refs_1_, bf16[3,512,1536]{2,1,0:T(8,128)(2,1)} %get-tuple-element.178.refs_2_, ...), custom_call_target="tpu_custom_call" | custom-call | tf_op jit(solution)/shard_map/steps/pallas_call | solution.py:250
  360.3 3.0 collective-permute-start.56
  363.3 23.6 %steps.8 = (f32[6,2,64,256]{3,2,1,0:T(8,128)}, f32[6,2,64,256]{3,2,1,0:T(8,128)}, f32[6,2,64,256]{3,2,1,0:T(8,128)}, f32[6,2,64,256]{3,2,1,0:T(8,128)}) custom-call(s32[1]{0:T(128)} %bitcast.refs_0_, f32[2,6]{1,0:T(2,128)} %get-tuple-element.273.refs_1_, bf16[3,512,1536]{2,1,0:T(8,128)(2,1)} %get-tuple-element.178.refs_2_, ...), custom_call_target="tpu_custom_call" | custom-call | tf_op jit(solution)/shard_map/steps/pallas_call | solution.py:250
  386.9 23.6 %steps.7 = (f32[6,2,64,256]{3,2,1,0:T(8,128)}, f32[6,2,64,256]{3,2,1,0:T(8,128)}, f32[6,2,64,256]{3,2,1,0:T(8,128)}, f32[6,2,64,256]{3,2,1,0:T(8,128)}) custom-call(s32[1]{0:T(128)} %bitcast.refs_0_, f32[2,6]{1,0:T(2,128)} %get-tuple-element.274.refs_1_, bf16[3,512,1536]{2,1,0:T(8,128)(2,1)} %get-tuple-element.178.refs_2_, ...), custom_call_target="tpu_custom_call" | custom-call | tf_op jit(solution)/shard_map/steps/pallas_call | solution.py:250
  411.2 4.5 broadcast_in_dim.2
  418.6 2.9 collective-permute-start.59
  424.4 2.7 collective-permute-done.68
  429.5 10.8 %collective-permute-done.57 = f32[3,2,64,256]{3,2,1,0:T(8,128)S(1)} collective-permute-done((f32[3,2,64,256]{3,2,1,0:T(8,128)S(1)}, f32[3,2,64,256]{3,2,1,0:T(8,128)S(1)}, u32[]{:S(2)}, u32[]{:S(2)}) %collective-permute-start.57) | collective-permute-done | bytes 393248 | tf_op jit(solution)/shard_map/ppermute | solution.py:72
  441.1 13.5 %collective-permute-done.58 = f32[3,2,64,256]{3,2,1,0:T(8,128)S(1)} collective-permute-done((f32[3,2,64,256]{3,2,1,0:T(8,128)S(1)}, f32[3,2,64,256]{3,2,1,0:T(8,128)S(1)}, u32[]{:S(2)}, u32[]{:S(2)}) %collective-permute-start.58) | collective-permute-done | bytes 393248 | tf_op jit(solution)/shard_map/ppermute | solution.py:72
  459.3 7.2 %steps.9 = (f32[1,2,64,256]{3,2,1,0:T(8,128)}, f32[1,2,64,256]{3,2,1,0:T(8,128)}, f32[1,2,64,256]{3,2,1,0:T(8,128)}, f32[1,2,64,256]{3,2,1,0:T(8,128)}) custom-call(s32[1]{0:T(128)} %bitcast.refs_0_, f32[2,1]{1,0:T(2,128)} %copy.43.refs_1_, bf16[3,512,1536]{2,1,0:T(8,128)(2,1)} %get-tuple-element.178.refs_2_, ...), custom_call_target="tpu_custom_call" | custom-call | tf_op jit(solution)/shard_map/steps/pallas_call | solution.py:250
  470.6 32.4 %collective-permute-done.60 = f32[6,2,64,256]{3,2,1,0:T(8,128)S(1)} collective-permute-done((f32[6,2,64,256]{3,2,1,0:T(8,128)}, f32[6,2,64,256]{3,2,1,0:T(8,128)S(1)}, u32[]{:S(2)}, u32[]{:S(2)}) %collective-permute-start.60) | collective-permute-done | bytes 786464 | tf_op jit(solution)/shard_map/ppermute | solution.py:72
  503.9 48.2 %collective-permute-done.61 = f32[6,2,64,256]{3,2,1,0:T(8,128)S(1)} collective-permute-done((f32[6,2,64,256]{3,2,1,0:T(8,128)}, f32[6,2,64,256]{3,2,1,0:T(8,128)S(1)}, u32[]{:S(2)}, u32[]{:S(2)}) %collective-permute-start.61) | collective-permute-done | bytes 786464 | tf_op jit(solution)/shard_map/ppermute | solution.py:72
  554.9 12.0 %collective-permute-done.63 = f32[6,2,64,256]{3,2,1,0:T(8,128)} collective-permute-done((f32[6,2,64,256]{3,2,1,0:T(8,128)}, f32[6,2,64,256]{3,2,1,0:T(8,128)}, u32[]{:S(2)}, u32[]{:S(2)}) %collective-permute-start.63) | collective-permute-done | bytes 786464 | tf_op jit(solution)/shard_map/ppermute | solution.py:72
  569.0 15.5 %collective-permute-done.64 = f32[6,2,64,256]{3,2,1,0:T(8,128)S(1)} collective-permute-done((f32[6,2,64,256]{3,2,1,0:T(8,128)}, f32[6,2,64,256]{3,2,1,0:T(8,128)S(1)}, u32[]{:S(2)}, u32[]{:S(2)}) %collective-permute-start.64) | collective-permute-done | bytes 786464 | tf_op jit(solution)/shard_map/ppermute | solution.py:72
  (313 shorter events, 117.3 us)
Async XLA Ops:
  14.2 20.7 %collective-permute-start.10 = (f32[512,128]{1,0:T(8,128)}, f32[512,128]{1,0:T(8,128)S(1)}, u32[]{:S(2)}, u32[]{:S(2)}) collective-permute-start(f32[512,128]{1,0:T(8,128)} %bitcast.295), channel_id=1, source_target_pairs={{0,16},{4,20},{8,24},{12,28},{16,0},{20,4},{24,8},{28,12},{1,17},{... | collective-permute-start | bytes 786440 | tf_op jit(solution)/shard_map/ppermute | solution.py:72
  15.8 23.7 %collective-permute-start.11 = (f32[512,128]{1,0:T(8,128)}, f32[512,128]{1,0:T(8,128)S(1)}, u32[]{:S(2)}, u32[]{:S(2)}) collective-permute-start(f32[512,128]{1,0:T(8,128)} %bitcast.294), channel_id=1, source_target_pairs={{0,20},{4,16},{8,28},{12,24},{16,4},{20,0},{24,12},{28,8},{1,21},{... | collective-permute-start | bytes 786440 | tf_op jit(solution)/shard_map/ppermute | solution.py:72
  16.1 26.7 %collective-permute-start.12 = (f32[512,128]{1,0:T(8,128)}, f32[512,128]{1,0:T(8,128)S(1)}, u32[]{:S(2)}, u32[]{:S(2)}) collective-permute-start(f32[512,128]{1,0:T(8,128)} %bitcast.293), channel_id=1, source_target_pairs={{0,24},{4,28},{8,16},{12,20},{16,8},{20,12},{24,0},{28,4},{1,25},{... | collective-permute-start | bytes 786440 | tf_op jit(solution)/shard_map/ppermute | solution.py:72
  17.6 25.2 %collective-permute-start.13 = (f32[512,128]{1,0:T(8,128)}, f32[512,128]{1,0:T(8,128)S(1)}, u32[]{:S(2)}, u32[]{:S(2)}) collective-permute-start(f32[512,128]{1,0:T(8,128)} %bitcast.292), channel_id=1, source_target_pairs={{0,28},{4,24},{8,20},{12,16},{16,12},{20,8},{24,4},{28,0},{1,29},{... | collective-permute-start | bytes 786440 | tf_op jit(solution)/shard_map/ppermute | solution.py:72
  18.7 24.1 %collective-permute-start.7 = (f32[512,128]{1,0:T(8,128)}, f32[512,128]{1,0:T(8,128)S(1)}, u32[]{:S(2)}, u32[]{:S(2)}) collective-permute-start(f32[512,128]{1,0:T(8,128)} %bitcast.291), channel_id=1, source_target_pairs={{0,4},{4,0},{8,12},{12,8},{16,20},{20,16},{24,28},{28,24},{1,5},{5... | collective-permute-start | bytes 786440 | tf_op jit(solution)/shard_map/ppermute | solution.py:72
  53.6 60.0 %all-to-all-start = ((f32[32,128,128]{2,1,0:T(8,128)}), f32[32,128,128]{2,1,0:T(8,128)S(1)}, u32[]{:S(2)}, u32[]{:S(2)}) async-start(f32[32,128,128]{2,1,0:T(8,128)} %bitcast.237), calls=%async_computation | async-start | bytes 4194304 | tf_op jit(solution)/shard_map/all_to_all | solution.py:382
  61.6 19.4 %collective-permute-start.16 = (f32[512,128]{1,0:T(8,128)}, f32[512,128]{1,0:T(8,128)S(1)}, u32[]{:S(2)}, u32[]{:S(2)}) collective-permute-start(f32[512,128]{1,0:T(8,128)} %bitcast.306), channel_id=1, source_target_pairs={{0,8},{4,12},{8,0},{12,4},{16,24},{20,28},{24,16},{28,20},{1,9},{5... | collective-permute-start | bytes 786440 | tf_op jit(solution)/shard_map/ppermute | solution.py:72
  63.1 25.6 %collective-permute-start.17 = (f32[512,128]{1,0:T(8,128)}, f32[512,128]{1,0:T(8,128)S(1)}, u32[]{:S(2)}, u32[]{:S(2)}) collective-permute-start(f32[512,128]{1,0:T(8,128)} %bitcast.304), channel_id=1, source_target_pairs={{0,12},{4,8},{8,4},{12,0},{16,28},{20,24},{24,20},{28,16},{1,13},{... | collective-permute-start | bytes 786440 | tf_op jit(solution)/shard_map/ppermute | solution.py:72
  63.4 25.3 %collective-permute-start.18 = (f32[512,128]{1,0:T(8,128)}, f32[512,128]{1,0:T(8,128)S(1)}, u32[]{:S(2)}, u32[]{:S(2)}) collective-permute-start(f32[512,128]{1,0:T(8,128)} %bitcast.302), channel_id=1, source_target_pairs={{0,16},{4,20},{8,24},{12,28},{16,0},{20,4},{24,8},{28,12},{1,17},{... | collective-permute-start | bytes 786440 | tf_op jit(solution)/shard_map/ppermute | solution.py:72
  64.8 23.9 %collective-permute-start.19 = (f32[512,128]{1,0:T(8,128)}, f32[512,128]{1,0:T(8,128)S(1)}, u32[]{:S(2)}, u32[]{:S(2)}) collective-permute-start(f32[512,128]{1,0:T(8,128)} %bitcast.300), channel_id=1, source_target_pairs={{0,20},{4,16},{8,28},{12,24},{16,4},{20,0},{24,12},{28,8},{1,21},{... | collective-permute-start | bytes 786440 | tf_op jit(solution)/shard_map/ppermute | solution.py:72
  65.1 36.8 %collective-permute-start.20 = (f32[512,128]{1,0:T(8,128)}, f32[512,128]{1,0:T(8,128)}, u32[]{:S(2)}, u32[]{:S(2)}) collective-permute-start(f32[512,128]{1,0:T(8,128)} %bitcast.298), channel_id=1, source_target_pairs={{0,24},{4,28},{8,16},{12,20},{16,8},{20,12},{24,0},{28,4},{1,25},{... | collective-permute-start | bytes 786440 | tf_op jit(solution)/shard_map/ppermute | solution.py:72
  81.0 26.9 %collective-permute-start.21 = (f32[512,128]{1,0:T(8,128)}, f32[512,128]{1,0:T(8,128)}, u32[]{:S(2)}, u32[]{:S(2)}) collective-permute-start(f32[512,128]{1,0:T(8,128)} %bitcast.296), channel_id=1, source_target_pairs={{0,28},{4,24},{8,20},{12,16},{16,12},{20,8},{24,4},{28,0},{1,29},{... | collective-permute-start | bytes 786440 | tf_op jit(solution)/shard_map/ppermute | solution.py:72
  114.9 59.6 %all-to-all-start.1 = ((f32[32,128,128]{2,1,0:T(8,128)}), f32[32,128,128]{2,1,0:T(8,128)}, u32[]{:S(2)}, u32[]{:S(2)}) async-start(f32[32,128,128]{2,1,0:T(8,128)} %bitcast.236), calls=%async_computation.1 | async-start | bytes 4194304 | tf_op jit(solution)/shard_map/all_to_all | solution.py:382
  122.0 19.4 %collective-permute-start.40 = (f32[512,128]{1,0:T(8,128)}, f32[512,128]{1,0:T(8,128)S(1)}, u32[]{:S(2)}, u32[]{:S(2)}) collective-permute-start(f32[512,128]{1,0:T(8,128)} %bitcast.307), channel_id=1, source_target_pairs={{0,8},{4,12},{8,0},{12,4},{16,24},{20,28},{24,16},{28,20},{1,9},{5... | collective-permute-start | bytes 786440 | tf_op jit(solution)/shard_map/ppermute | solution.py:72
  123.4 25.6 %collective-permute-start.41 = (f32[512,128]{1,0:T(8,128)}, f32[512,128]{1,0:T(8,128)S(1)}, u32[]{:S(2)}, u32[]{:S(2)}) collective-permute-start(f32[512,128]{1,0:T(8,128)} %bitcast.305), channel_id=1, source_target_pairs={{0,12},{4,8},{8,4},{12,0},{16,28},{20,24},{24,20},{28,16},{1,13},{... | collective-permute-start | bytes 786440 | tf_op jit(solution)/shard_map/ppermute | solution.py:72
  123.7 25.3 %collective-permute-start.42 = (f32[512,128]{1,0:T(8,128)}, f32[512,128]{1,0:T(8,128)S(1)}, u32[]{:S(2)}, u32[]{:S(2)}) collective-permute-start(f32[512,128]{1,0:T(8,128)} %bitcast.303), channel_id=1, source_target_pairs={{0,16},{4,20},{8,24},{12,28},{16,0},{20,4},{24,8},{28,12},{1,17},{... | collective-permute-start | bytes 786440 | tf_op jit(solution)/shard_map/ppermute | solution.py:72
  125.2 23.9 %collective-permute-start.43 = (f32[512,128]{1,0:T(8,128)}, f32[512,128]{1,0:T(8,128)S(1)}, u32[]{:S(2)}, u32[]{:S(2)}) collective-permute-start(f32[512,128]{1,0:T(8,128)} %bitcast.301), channel_id=1, source_target_pairs={{0,20},{4,16},{8,28},{12,24},{16,4},{20,0},{24,12},{28,8},{1,21},{... | collective-permute-start | bytes 786440 | tf_op jit(solution)/shard_map/ppermute | solution.py:72
  125.5 36.7 %collective-permute-start.44 = (f32[512,128]{1,0:T(8,128)}, f32[512,128]{1,0:T(8,128)S(1)}, u32[]{:S(2)}, u32[]{:S(2)}) collective-permute-start(f32[512,128]{1,0:T(8,128)} %bitcast.299), channel_id=1, source_target_pairs={{0,24},{4,28},{8,16},{12,20},{16,8},{20,12},{24,0},{28,4},{1,25},{... | collective-permute-start | bytes 786440 | tf_op jit(solution)/shard_map/ppermute | solution.py:72
  141.4 26.8 %collective-permute-start.45 = (f32[512,128]{1,0:T(8,128)}, f32[512,128]{1,0:T(8,128)S(1)}, u32[]{:S(2)}, u32[]{:S(2)}) collective-permute-start(f32[512,128]{1,0:T(8,128)} %bitcast.297), channel_id=1, source_target_pairs={{0,28},{4,24},{8,20},{12,16},{16,12},{20,8},{24,4},{28,0},{1,29},{... | collective-permute-start | bytes 786440 | tf_op jit(solution)/shard_map/ppermute | solution.py:72
  174.5 101.1 %all-to-all-start.2 = ((f32[32,128,128]{2,1,0:T(8,128)}), f32[32,128,128]{2,1,0:T(8,128)S(1)}, u32[]{:S(2)}, u32[]{:S(2)}) async-start(f32[32,128,128]{2,1,0:T(8,128)} %bitcast.234), calls=%async_computation.2 | async-start | bytes 4194304 | tf_op jit(solution)/shard_map/all_to_all | solution.py:382
  194.8 22.7 %collective-permute-start.4 = (f32[2,2,32,256]{3,2,1,0:T(8,128)S(1)}, f32[2,2,32,256]{3,2,1,0:T(8,128)S(1)}, u32[]{:S(2)}, u32[]{:S(2)}) collective-permute-start(f32[2,2,32,256]{3,2,1,0:T(8,128)S(1)} %fusion.4), channel_id=1, source_target_pairs={{0,1},{1,0},{2,3},{3,2},{4,5},{5,4},{6,7},{7,6},{8,9},{9,8},{10,11... | collective-permute-start | bytes 393224 | tf_op jit(solution)/shard_map/ppermute | solution.py:72
  197.4 36.8 %collective-permute-start.5 = (f32[2,2,32,256]{3,2,1,0:T(8,128)S(1)}, f32[2,2,32,256]{3,2,1,0:T(8,128)S(1)}, u32[]{:S(2)}, u32[]{:S(2)}) collective-permute-start(f32[2,2,32,256]{3,2,1,0:T(8,128)S(1)} %fusion.4), channel_id=1, source_target_pairs={{0,2},{1,3},{2,0},{3,1},{4,6},{5,7},{6,4},{7,5},{8,10},{9,11},{10,... | collective-permute-start | bytes 393224 | tf_op jit(solution)/shard_map/ppermute | solution.py:72
  201.6 37.2 %collective-permute-start.6 = (f32[2,2,32,256]{3,2,1,0:T(8,128)S(1)}, f32[2,2,32,256]{3,2,1,0:T(8,128)S(1)}, u32[]{:S(2)}, u32[]{:S(2)}) collective-permute-start(f32[2,2,32,256]{3,2,1,0:T(8,128)S(1)} %fusion.4), channel_id=1, source_target_pairs={{0,3},{1,2},{2,1},{3,0},{4,7},{5,6},{6,5},{7,4},{8,11},{9,10},{10,... | collective-permute-start | bytes 393224 | tf_op jit(solution)/shard_map/ppermute | solution.py:72
  202.2 38.5 %collective-permute-start.29 = (f32[2,8,256]{2,1,0:T(8,128)S(1)}, f32[2,8,256]{2,1,0:T(8,128)S(1)}, u32[]{:S(2)}, u32[]{:S(2)}) collective-permute-start(f32[2,8,256]{2,1,0:T(8,128)S(1)} %add_add_fusion), channel_id=1, source_target_pairs={{0,1},{1,0},{2,3},{3,2},{4,5},{5,4},{6,7},{7,6},{8,9},{9,8},{10,11... | collective-permute-start | bytes 49160 | tf_op jit(solution)/shard_map/ppermute | solution.py:72
  203.6 37.8 %collective-permute-start.30 = (f32[2,8,256]{2,1,0:T(8,128)S(1)}, f32[2,8,256]{2,1,0:T(8,128)S(1)}, u32[]{:S(2)}, u32[]{:S(2)}) collective-permute-start(f32[2,8,256]{2,1,0:T(8,128)S(1)} %add_add_fusion), channel_id=1, source_target_pairs={{0,2},{1,3},{2,0},{3,1},{4,6},{5,7},{6,4},{7,5},{8,10},{9,11},{10,... | collective-permute-start | bytes 49160 | tf_op jit(solution)/shard_map/ppermute | solution.py:72
  217.5 25.5 %collective-permute-start.31 = (f32[2,8,256]{2,1,0:T(8,128)S(1)}, f32[2,8,256]{2,1,0:T(8,128)S(1)}, u32[]{:S(2)}, u32[]{:S(2)}) collective-permute-start(f32[2,8,256]{2,1,0:T(8,128)S(1)} %add_add_fusion), channel_id=1, source_target_pairs={{0,3},{1,2},{2,1},{3,0},{4,7},{5,6},{6,5},{7,4},{8,11},{9,10},{10,... | collective-permute-start | bytes 49160 | tf_op jit(solution)/shard_map/ppermute | solution.py:72
  243.0 37.2 %collective-permute-start.14 = (f32[4,2,2,32,256]{4,3,2,1,0:T(8,128)S(1)}, f32[4,2,2,32,256]{4,3,2,1,0:T(8,128)S(1)}, u32[]{:S(2)}, u32[]{:S(2)}) collective-permute-start(f32[4,2,2,32,256]{4,3,2,1,0:T(8,128)S(1)} %fusion.3), channel_id=1, source_target_pairs={{0,4},{4,0},{8,12},{12,8},{16,20},{20,16},{24,28},{28,24},{1,5},{5... | collective-permute-start | bytes 1572872 | tf_op jit(solution)/shard_map/ppermute | solution.py:72
  243.5 23.4 %collective-permute-start.50 = (f32[512,128]{1,0:T(8,128)S(1)}, f32[512,128]{1,0:T(8,128)S(1)}, u32[]{:S(2)}, u32[]{:S(2)}) collective-permute-start(f32[512,128]{1,0:T(8,128)S(1)} %bitcast.285), channel_id=1, source_target_pairs={{0,20},{4,16},{8,28},{12,24},{16,4},{20,0},{24,12},{28,8},{1,21},{... | collective-permute-start | bytes 786440 | tf_op jit(solution)/shard_map/ppermute | solution.py:72
  248.2 20.0 %collective-permute-start.51 = (f32[512,128]{1,0:T(8,128)S(1)}, f32[512,128]{1,0:T(8,128)S(1)}, u32[]{:S(2)}, u32[]{:S(2)}) collective-permute-start(f32[512,128]{1,0:T(8,128)S(1)} %bitcast.284), channel_id=1, source_target_pairs={{0,24},{4,28},{8,16},{12,20},{16,8},{20,12},{24,0},{28,4},{1,25},{... | collective-permute-start | bytes 786440 | tf_op jit(solution)/shard_map/ppermute | solution.py:72
  255.9 25.6 %collective-permute-start.32 = (f32[4,2,8,256]{3,2,0,1:T(8,128)S(1)}, f32[4,2,8,256]{3,2,0,1:T(8,128)S(1)}, u32[]{:S(2)}, u32[]{:S(2)}) collective-permute-start(f32[4,2,8,256]{3,2,0,1:T(8,128)S(1)} %select_select_fusion.3), channel_id=1, source_target_pairs={{0,4},{4,0},{8,12},{12,8},{16,20},{20,16},{24,28},{28,24},{1,5},{5... | collective-permute-start | bytes 196616 | tf_op jit(solution)/shard_map/ppermute | solution.py:72
  268.2 17.3 %collective-permute-start.34 = (f32[4,2,8,256]{3,2,0,1:T(8,128)S(1)}, f32[4,2,8,256]{3,2,0,1:T(8,128)}, u32[]{:S(2)}, u32[]{:S(2)}) collective-permute-start(f32[4,2,8,256]{3,2,0,1:T(8,128)S(1)} %select_select_fusion.3), channel_id=1, source_target_pairs={{0,12},{4,8},{8,4},{12,0},{16,28},{20,24},{24,20},{28,16},{1,13},{... | collective-permute-start | bytes 196616 | tf_op jit(solution)/shard_map/ppermute | solution.py:72
  268.4 17.0 %collective-permute-start.35 = (f32[4,2,8,256]{3,2,0,1:T(8,128)S(1)}, f32[4,2,8,256]{3,2,0,1:T(8,128)}, u32[]{:S(2)}, u32[]{:S(2)}) collective-permute-start(f32[4,2,8,256]{3,2,0,1:T(8,128)S(1)} %select_select_fusion.3), channel_id=1, source_target_pairs={{0,16},{4,20},{8,24},{12,28},{16,0},{20,4},{24,8},{28,12},{1,17},{... | collective-permute-start | bytes 196616 | tf_op jit(solution)/shard_map/ppermute | solution.py:72
  276.9 52.0 %all-to-all-start.3 = ((f32[32,128,128]{2,1,0:T(8,128)}), f32[32,128,128]{2,1,0:T(8,128)}, u32[]{:S(2)}, u32[]{:S(2)}) async-start(f32[32,128,128]{2,1,0:T(8,128)} %bitcast.235), calls=%async_computation.3 | async-start | bytes 4194304 | tf_op jit(solution)/shard_map/all_to_all | solution.py:382
  280.2 17.5 %collective-permute-start.36 = (f32[4,2,8,256]{3,2,0,1:T(8,128)S(1)}, f32[4,2,8,256]{3,2,0,1:T(8,128)S(1)}, u32[]{:S(2)}, u32[]{:S(2)}) collective-permute-start(f32[4,2,8,256]{3,2,0,1:T(8,128)S(1)} %select_select_fusion.3), channel_id=1, source_target_pairs={{0,20},{4,16},{8,28},{12,24},{16,4},{20,0},{24,12},{28,8},{1,21},{... | collective-permute-start | bytes 196616 | tf_op jit(solution)/shard_map/ppermute | solution.py:72
  281.5 17.7 %collective-permute-start.37 = (f32[4,2,8,256]{3,2,0,1:T(8,128)S(1)}, f32[4,2,8,256]{3,2,0,1:T(8,128)S(1)}, u32[]{:S(2)}, u32[]{:S(2)}) collective-permute-start(f32[4,2,8,256]{3,2,0,1:T(8,128)S(1)} %select_select_fusion.3), channel_id=1, source_target_pairs={{0,24},{4,28},{8,16},{12,20},{16,8},{20,12},{24,0},{28,4},{1,25},{... | collective-permute-start | bytes 196616 | tf_op jit(solution)/shard_map/ppermute | solution.py:72
  340.8 69.7 %collective-permute-start.66 = (f32[2,4,8,128]{3,2,1,0:T(8,128)S(1)}, f32[2,4,8,128]{3,2,1,0:T(8,128)S(1)}, u32[]{:S(2)}, u32[]{:S(2)}) collective-permute-start(f32[2,4,8,128]{3,2,1,0:T(8,128)S(1)} %pad_maximum_fusion.17), channel_id=1, source_target_pairs={{0,1},{1,0},{2,3},{3,2},{4,5},{5,4},{6,7},{7,6},{8,9},{9,8},{10,11... | collective-permute-start | bytes 98312 | tf_op jit(solution)/shard_map/ppermute | solution.py:72
  343.0 73.7 %collective-permute-start.53 = (f32[1,2,64,256]{3,2,1,0:T(8,128)}, f32[1,2,64,256]{3,2,1,0:T(8,128)S(1)}, u32[]{:S(2)}, u32[]{:S(2)}) collective-permute-start(f32[1,2,64,256]{3,2,1,0:T(8,128)} %get-tuple-element.192), channel_id=1, source_target_pairs={{0,1},{1,0},{2,3},{3,2},{4,5},{5,4},{6,7},{7,6},{8,9},{9,8},{10,11... | collective-permute-start | bytes 393224 | tf_op jit(solution)/shard_map/ppermute | solution.py:72
  345.0 73.6 %collective-permute-start.54 = (f32[1,2,64,256]{3,2,1,0:T(8,128)}, f32[1,2,64,256]{3,2,1,0:T(8,128)S(1)}, u32[]{:S(2)}, u32[]{:S(2)}) collective-permute-start(f32[1,2,64,256]{3,2,1,0:T(8,128)} %get-tuple-element.193), channel_id=1, source_target_pairs={{0,2},{1,3},{2,0},{3,1},{4,6},{5,7},{6,4},{7,5},{8,10},{9,11},{10,... | collective-permute-start | bytes 393224 | tf_op jit(solution)/shard_map/ppermute | solution.py:72
  345.2 77.0 %collective-permute-start.55 = (f32[1,2,64,256]{3,2,1,0:T(8,128)}, f32[1,2,64,256]{3,2,1,0:T(8,128)S(1)}, u32[]{:S(2)}, u32[]{:S(2)}) collective-permute-start(f32[1,2,64,256]{3,2,1,0:T(8,128)} %get-tuple-element.194), channel_id=1, source_target_pairs={{0,3},{1,2},{2,1},{3,0},{4,7},{5,6},{6,5},{7,4},{8,11},{9,10},{10,... | collective-permute-start | bytes 393224 | tf_op jit(solution)/shard_map/ppermute | solution.py:72
  360.3 66.9 %collective-permute-start.56 = (f32[3,2,64,256]{3,2,1,0:T(8,128)}, f32[3,2,64,256]{3,2,1,0:T(8,128)S(1)}, u32[]{:S(2)}, u32[]{:S(2)}) collective-permute-start(f32[3,2,64,256]{3,2,1,0:T(8,128)} %get-tuple-element.196), channel_id=1, source_target_pairs={{0,1},{1,0},{2,3},{3,2},{4,5},{5,4},{6,7},{7,6},{8,9},{9,8},{10,11... | collective-permute-start | bytes 1179656 | tf_op jit(solution)/shard_map/ppermute | solution.py:72
  416.3 24.0 %collective-permute-start.57 = (f32[3,2,64,256]{3,2,1,0:T(8,128)S(1)}, f32[3,2,64,256]{3,2,1,0:T(8,128)S(1)}, u32[]{:S(2)}, u32[]{:S(2)}) collective-permute-start(f32[3,2,64,256]{3,2,1,0:T(8,128)S(1)} %copy-done.43), channel_id=1, source_target_pairs={{0,2},{1,3},{2,0},{3,1},{4,6},{5,7},{6,4},{7,5},{8,10},{9,11},{10,... | collective-permute-start | bytes 1179656 | tf_op jit(solution)/shard_map/ppermute | solution.py:72
  416.7 37.9 %collective-permute-start.58 = (f32[3,2,64,256]{3,2,1,0:T(8,128)S(1)}, f32[3,2,64,256]{3,2,1,0:T(8,128)S(1)}, u32[]{:S(2)}, u32[]{:S(2)}) collective-permute-start(f32[3,2,64,256]{3,2,1,0:T(8,128)S(1)} %copy-done.42), channel_id=1, source_target_pairs={{0,3},{1,2},{2,1},{3,0},{4,7},{5,6},{6,5},{7,4},{8,11},{9,10},{10,... | collective-permute-start | bytes 1179656 | tf_op jit(solution)/shard_map/ppermute | solution.py:72
  418.6 49.5 %collective-permute-start.59 = (f32[6,2,64,256]{3,2,1,0:T(8,128)}, f32[6,2,64,256]{3,2,1,0:T(8,128)S(1)}, u32[]{:S(2)}, u32[]{:S(2)}) collective-permute-start(f32[6,2,64,256]{3,2,1,0:T(8,128)} %get-tuple-element.200), channel_id=1, source_target_pairs={{0,1},{1,0},{2,3},{3,2},{4,5},{5,4},{6,7},{7,6},{8,9},{9,8},{10,11... | collective-permute-start | bytes 2359304 | tf_op jit(solution)/shard_map/ppermute | solution.py:72
  427.2 75.8 %collective-permute-start.60 = (f32[6,2,64,256]{3,2,1,0:T(8,128)}, f32[6,2,64,256]{3,2,1,0:T(8,128)S(1)}, u32[]{:S(2)}, u32[]{:S(2)}) collective-permute-start(f32[6,2,64,256]{3,2,1,0:T(8,128)} %get-tuple-element.201), channel_id=1, source_target_pairs={{0,2},{1,3},{2,0},{3,1},{4,6},{5,7},{6,4},{7,5},{8,10},{9,11},{10,... | collective-permute-start | bytes 2359304 | tf_op jit(solution)/shard_map/ppermute | solution.py:72
  427.2 124.8 %collective-permute-start.61 = (f32[6,2,64,256]{3,2,1,0:T(8,128)}, f32[6,2,64,256]{3,2,1,0:T(8,128)S(1)}, u32[]{:S(2)}, u32[]{:S(2)}) collective-permute-start(f32[6,2,64,256]{3,2,1,0:T(8,128)} %get-tuple-element.202), channel_id=1, source_target_pairs={{0,3},{1,2},{2,1},{3,0},{4,7},{5,6},{6,5},{7,4},{8,11},{9,10},{10,... | collective-permute-start | bytes 2359304 | tf_op jit(solution)/shard_map/ppermute | solution.py:72
  454.6 99.3 %collective-permute-start.62 = (f32[6,2,64,256]{3,2,1,0:T(8,128)}, f32[6,2,64,256]{3,2,1,0:T(8,128)S(1)}, u32[]{:S(2)}, u32[]{:S(2)}) collective-permute-start(f32[6,2,64,256]{3,2,1,0:T(8,128)} %get-tuple-element.204), channel_id=1, source_target_pairs={{0,1},{1,0},{2,3},{3,2},{4,5},{5,4},{6,7},{7,6},{8,9},{9,8},{10,11... | collective-permute-start | bytes 2359304 | tf_op jit(solution)/shard_map/ppermute | solution.py:72
  456.3 110.6 %collective-permute-start.63 = (f32[6,2,64,256]{3,2,1,0:T(8,128)}, f32[6,2,64,256]{3,2,1,0:T(8,128)}, u32[]{:S(2)}, u32[]{:S(2)}) collective-permute-start(f32[6,2,64,256]{3,2,1,0:T(8,128)} %get-tuple-element.205), channel_id=1, source_target_pairs={{0,2},{1,3},{2,0},{3,1},{4,6},{5,7},{6,4},{7,5},{8,10},{9,11},{10,... | collective-permute-start | bytes 2359304 | tf_op jit(solution)/shard_map/ppermute | solution.py:72
  468.1 116.4 %collective-permute-start.64 = (f32[6,2,64,256]{3,2,1,0:T(8,128)}, f32[6,2,64,256]{3,2,1,0:T(8,128)S(1)}, u32[]{:S(2)}, u32[]{:S(2)}) collective-permute-start(f32[6,2,64,256]{3,2,1,0:T(8,128)} %get-tuple-element.206), channel_id=1, source_target_pairs={{0,3},{1,2},{2,1},{3,0},{4,7},{5,6},{6,5},{7,4},{8,11},{9,10},{10,... | collective-permute-start | bytes 2359304 | tf_op jit(solution)/shard_map/ppermute | solution.py:72
  (76 other events, 833.7 us)
where the time goes:
time: 587 us; the launch traced here: 585 us
  waiting for transfers between devices  322 us (55%)
  Pallas kernels  120 us (20%)
  starting transfers between devices  94.8 us (16%)
  local copies, waits for them, and re-layouts  31.2 us (5%)
  other arithmetic  13.6 us (2%)
    ppermute x70, waiting for transfers between devices, swap(): lax.ppermute(array, axis, [(i, i ^ offset) for i in range(lax.axis_size(a...  310 us
    ppermute x70, starting transfers between devices, swap(): lax.ppermute(array, axis, [(i, i ^ offset) for i in range(lax.axis_size(a...  77.4 us
    pallas_call x5, Pallas kernels, steps(): pl.pallas_call(lambda *refs: steps_kernel(groups, rings, blocks, *refs),...  75.4 us
    pallas_call x4, Pallas kernels, mix(): pl.pallas_call(mix_kernel, out_shape=(jax.ShapeDtypeStruct((groups * leng...  22.4 us
    all_to_all x4, starting transfers between devices, on_device(): wholes.append(lax.all_to_all(mixed, ('mode', 'orb'), 0, 0, tiled=True))  17.5 us
    dynamic_update_slice x16, local copies, waits for them, and re-layouts, on_device(): lax.dynamic_update_slice(stacks, part, ((ring ^ k) * owned + first, 0, 0,...  14.4 us
    pallas_call x1, Pallas kernels, tables(): pl.pallas_call(densities_kernel, out_shape=(jax.ShapeDtypeStruct((3, 2 *...  12.8 us
    all_to_all x4, waiting for transfers between devices, on_device(): wholes.append(lax.all_to_all(mixed, ('mode', 'orb'), 0, 0, tiled=True))  12 us
  transfers between devices with their start and end apart: 74, of which 34 were waited for; matrix products, arithmetic and copies ran while one was open for 7% of the time, Pallas kernels for 18%

commit v1 on v0

--- a/solution.py
+++ b/solution.py
@@ -8,7 +8,7 @@
 time_step = 0.1
 field_weight = 0.0625
 tile_rows, tile_cols = 8, 128
-out_shares = (1, 3, 6, 6)
+out_shares = (2, 3, 5, 6)
 
 
 def contract(form, first, second):
@@ -371,7 +371,7 @@
     share = rows // groups
     count = len(blocks)
     packed = [pack(here, flat, groups, depth, *blocks[0])]
-    packed.append(pack(here, after(flat, packed[0][0]), groups, depth, *blocks[1]))
+    packed.append(pack(here, after(flat, (packed[0][0], high)), groups, depth, *blocks[1]))
     wholes, sums, mixes = [], {}, []
     for turn, (b, h) in enumerate(blocks):
         pieces = exchange([piece.reshape(-1, tile_cols) for piece in packed[turn]], "mode")
@@ -407,6 +407,8 @@
             both = jnp.moveaxis(both, 0, 2).reshape(2, 2, order, order)
         if turn == 3:
             coupled = by_place(after(tuple(coupled), wholes[2]), place)
+    summed = jnp.stack([sums[block] for block in blocks])
+    summed = tuple(exchange([summed] * rings, "orb"))
     coupled = coupled.transpose(2, 1, 0, 3, 4).reshape(2, order, order)
     left, right, source, dens2 = tables(norm.reshape(1), both, coupled)
     own_coupling = lax.dynamic_slice_in_dim(coupling, ring * owned, owned, 0)
@@ -417,19 +419,19 @@
     first, finished = 0, []
     for share in out_shares:
         chunk = share * owned // sum(out_shares)
+        turn = ring.reshape(1)
         parts = steps(
-            ring.reshape(1), scales[:, first : first + chunk], left, right, source, dens2,
-            wholes, blocks, groups, rings, first, chunk,
+            after(turn, finished[-1]) if finished else turn, scales[:, first : first + chunk],
+            left, right, source, dens2, wholes, blocks, groups, rings, first, chunk,
         )
         finished.append(parts[0])
+        parts = exchange(parts, "orb")
         for k, part in enumerate(parts):
-            part = swap(part, "orb", k) if k else part
             stacks = lax.dynamic_update_slice(stacks, part, ((ring ^ k) * owned + first, 0, 0, 0))
         first += chunk
 
-    summed = jnp.stack([sums[block] for block in blocks])
-    summed = gather_by_doubling(after(summed, finished[0]), "orb")
-    summed = gather_by_doubling(after(summed, finished[-1]), "mode")
+    summed = by_place(after(summed, finished[-1]), ring)
+    summed = gather_by_doubling(summed, "mode")
     summed = summed.reshape((groups * rings,) + summed.shape[2:])
     scales = jnp.stack([norm_mixed, time_step * norm]).reshape(2, 1)
     parts = steps(

time: 587 us -> 589 us (level)
  the two profiles are of different devices: /device:TPU:8 before, /device:TPU:16 now
where the time goes in v1:
time: 589 us; the launch traced here: 588 us
  waiting for transfers between devices  324 us (55%)
  Pallas kernels  121 us (21%)
  starting transfers between devices  96.3 us (16%)
  local copies, waits for them, and re-layouts  30.7 us (5%)
  other arithmetic  13.4 us (2%)
    ppermute x71, waiting for transfers between devices, swap(): lax.ppermute(array, axis, [(i, i ^ offset) for i in range(lax.axis_size(a...  311 us
    ppermute x71, starting transfers between devices, swap(): lax.ppermute(array, axis, [(i, i ^ offset) for i in range(lax.axis_size(a...  77.5 us
    pallas_call x5, Pallas kernels, steps(): pl.pallas_call(lambda *refs: steps_kernel(groups, rings, blocks, *refs),...  75.8 us
    pallas_call x4, Pallas kernels, mix(): pl.pallas_call(mix_kernel, out_shape=(jax.ShapeDtypeStruct((groups * leng...  22.5 us
    all_to_all x4, starting transfers between devices, on_device(): wholes.append(lax.all_to_all(mixed, ('mode', 'orb'), 0, 0, tiled=True))  18.8 us
    dynamic_update_slice x16, local copies, waits for them, and re-layouts, on_device(): lax.dynamic_update_slice(stacks, part, ((ring ^ k) * owned + first, 0, 0,...  13.3 us
    pallas_call x1, Pallas kernels, tables(): pl.pallas_call(densities_kernel, out_shape=(jax.ShapeDtypeStruct((3, 2 *...  12.7 us
    all_to_all x4, waiting for transfers between devices, on_device(): wholes.append(lax.all_to_all(mixed, ('mode', 'orb'), 0, 0, tiled=True))  12.6 us
  transfers between devices with their start and end apart: 75, of which 34 were waited for; matrix products, arithmetic and copies ran while one was open for 6% of the time, Pallas kernels for 20%

profile of v1, /device:TPU:16, one launch (start us, length us, event | category | flops | bytes accessed | tf_op | source)
XLA Modules:
  0.0 588.4 jit_solution(5810557554065233437)
XLA Ops:
  8.0 3.6 collective-permute-done.1
  21.8 13.1 %collective-permute-done.10.refs_4_ = f32[512,128]{1,0:T(8,128)S(1)} collective-permute-done((f32[512,128]{1,0:T(8,128)}, f32[512,128]{1,0:T(8,128)S(1)}, u32[]{:S(2)}, u32[]{:S(2)}) %collective-permute-start.10) | collective-permute-done | bytes 262176 | tf_op jit(solution)/shard_map/ppermute | solution.py:72
  36.1 3.3 collective-permute-done.11.refs_5_
  42.8 4.4 collective-permute-done.9.refs_3_
  48.0 5.6 mix.4
  53.6 5.2 all-to-all-start
  67.4 13.9 %collective-permute-done.16.refs_2_ = f32[512,128]{1,0:T(8,128)S(1)} collective-permute-done((f32[512,128]{1,0:T(8,128)}, f32[512,128]{1,0:T(8,128)S(1)}, u32[]{:S(2)}, u32[]{:S(2)}) %collective-permute-start.16) | collective-permute-done | bytes 262176 | tf_op jit(solution)/shard_map/ppermute | solution.py:72
  81.3 7.5 %collective-permute-done.17.refs_3_ = f32[512,128]{1,0:T(8,128)S(1)} collective-permute-done((f32[512,128]{1,0:T(8,128)}, f32[512,128]{1,0:T(8,128)S(1)}, u32[]{:S(2)}, u32[]{:S(2)}) %collective-permute-start.17) | collective-permute-done | bytes 262176 | tf_op jit(solution)/shard_map/ppermute | solution.py:72
  88.9 3.3 collective-permute-done.19.refs_5_
  92.2 8.5 %collective-permute-done.20.refs_6_ = f32[512,128]{1,0:T(8,128)} collective-permute-done((f32[512,128]{1,0:T(8,128)}, f32[512,128]{1,0:T(8,128)}, u32[]{:S(2)}, u32[]{:S(2)}) %collective-permute-start.20) | collective-permute-done | bytes 262176 | tf_op jit(solution)/shard_map/ppermute | solution.py:72
  100.6 6.9 %collective-permute-done.21.refs_7_ = f32[512,128]{1,0:T(8,128)} collective-permute-done((f32[512,128]{1,0:T(8,128)}, f32[512,128]{1,0:T(8,128)}, u32[]{:S(2)}, u32[]{:S(2)}) %collective-permute-start.21) | collective-permute-done | bytes 262176 | tf_op jit(solution)/shard_map/ppermute | solution.py:72
  107.6 5.7 mix.5
  114.6 4.7 all-to-all-start.1
  127.8 13.9 %collective-permute-done.40.refs_2_ = f32[512,128]{1,0:T(8,128)S(1)} collective-permute-done((f32[512,128]{1,0:T(8,128)}, f32[512,128]{1,0:T(8,128)S(1)}, u32[]{:S(2)}, u32[]{:S(2)}) %collective-permute-start.40) | collective-permute-done | bytes 262176 | tf_op jit(solution)/shard_map/ppermute | solution.py:72
  141.7 7.5 %collective-permute-done.41.refs_3_ = f32[512,128]{1,0:T(8,128)S(1)} collective-permute-done((f32[512,128]{1,0:T(8,128)}, f32[512,128]{1,0:T(8,128)S(1)}, u32[]{:S(2)}, u32[]{:S(2)}) %collective-permute-start.41) | collective-permute-done | bytes 262176 | tf_op jit(solution)/shard_map/ppermute | solution.py:72
  149.3 3.3 collective-permute-done.43.refs_5_
  152.5 8.4 %collective-permute-done.44.refs_6_ = f32[512,128]{1,0:T(8,128)S(1)} collective-permute-done((f32[512,128]{1,0:T(8,128)}, f32[512,128]{1,0:T(8,128)S(1)}, u32[]{:S(2)}, u32[]{:S(2)}) %collective-permute-start.44) | collective-permute-done | bytes 262176 | tf_op jit(solution)/shard_map/ppermute | solution.py:72
  160.9 6.9 %collective-permute-done.45.refs_7_ = f32[512,128]{1,0:T(8,128)S(1)} collective-permute-done((f32[512,128]{1,0:T(8,128)}, f32[512,128]{1,0:T(8,128)S(1)}, u32[]{:S(2)}, u32[]{:S(2)}) %collective-permute-start.45) | collective-permute-done | bytes 262176 | tf_op jit(solution)/shard_map/ppermute | solution.py:72
  168.5 5.6 mix.6
  174.2 4.7 all-to-all-start.2
  179.0 4.3 multiply_reduce_fusion
  196.4 6.0 %collective-permute-start.4 = (f32[2,2,32,256]{3,2,1,0:T(8,128)S(1)}, f32[2,2,32,256]{3,2,1,0:T(8,128)S(1)}, u32[]{:S(2)}, u32[]{:S(2)}) collective-permute-start(f32[2,2,32,256]{3,2,1,0:T(8,128)S(1)} %fusion.4), channel_id=1, source_target_pairs={{0,1},{1,0},{2,3},{3,2},{4,5},{5,4},{6,7},{7,6},{8,9},{9,8},{10,11... | collective-permute-start | bytes 393224 | tf_op jit(solution)/shard_map/ppermute | solution.py:72
  204.0 2.9 collective-permute-start.29
  206.9 11.6 %collective-permute-done.4 = f32[2,2,32,256]{3,2,1,0:T(8,128)S(1)} collective-permute-done((f32[2,2,32,256]{3,2,1,0:T(8,128)S(1)}, f32[2,2,32,256]{3,2,1,0:T(8,128)S(1)}, u32[]{:S(2)}, u32[]{:S(2)}) %collective-permute-start.4) | collective-permute-done | bytes 131104 | tf_op jit(solution)/shard_map/ppermute | solution.py:72
  218.5 15.7 %collective-permute-done.5 = f32[2,2,32,256]{3,2,1,0:T(8,128)S(1)} collective-permute-done((f32[2,2,32,256]{3,2,1,0:T(8,128)S(1)}, f32[2,2,32,256]{3,2,1,0:T(8,128)S(1)}, u32[]{:S(2)}, u32[]{:S(2)}) %collective-permute-start.5) | collective-permute-done | bytes 131104 | tf_op jit(solution)/shard_map/ppermute | solution.py:72
  234.2 3.5 collective-permute-done.6
  242.7 4.3 collective-permute-done.47.refs_2_
  251.7 3.1 collective-permute-start.52
  254.9 10.9 %collective-permute-done.50.refs_5_ = f32[512,128]{1,0:T(8,128)S(1)} collective-permute-done((f32[512,128]{1,0:T(8,128)S(1)}, f32[512,128]{1,0:T(8,128)S(1)}, u32[]{:S(2)}, u32[]{:S(2)}) %collective-permute-start.50) | collective-permute-done | bytes 262176 | tf_op jit(solution)/shard_map/ppermute | solution.py:72
  268.9 5.6 mix.7
  275.8 4.2 all-to-all-start.3
  287.4 8.1 %collective-permute-done.36 = f32[4,2,8,256]{3,2,0,1:T(8,128)S(1)} collective-permute-done((f32[4,2,8,256]{3,2,0,1:T(8,128)S(1)}, f32[4,2,8,256]{3,2,0,1:T(8,128)S(1)}, u32[]{:S(2)}, u32[]{:S(2)}) %collective-permute-start.36) | collective-permute-done | bytes 65568 | tf_op jit(solution)/shard_map/ppermute | solution.py:72
  302.4 12.7 %densities.1 = (bf16[3,512,1536]{2,1,0:T(8,128)(2,1)}, bf16[3,1536,512]{2,1,0:T(8,128)(2,1)}, f32[2,256,256]{2,1,0:T(8,128)}, f32[2,256,256]{2,1,0:T(8,128)}) custom-call(f32[1]{0:T(128)} %bitcast.18.norm_ref, f32[2,2,256,256]{3,2,1,0:T(8,128)} %bitcast.242, f32[2,256,256]{2,1,0:T(8,128)} %bitcast.250), custom_call_target="tpu_custom_call" | custom-call | tf_op jit(solution)/shard_map/densities/pallas_call | solution.py:322
  315.0 12.6 %all-to-all-done.3.refs_9_ = f32[32,128,128]{2,1,0:T(8,128)} async-done(((f32[32,128,128]{2,1,0:T(8,128)}), f32[32,128,128]{2,1,0:T(8,128)}, u32[]{:S(2)}, u32[]{:S(2)}) %all-to-all-start.3) | async-done | bytes 2097184 | tf_op jit(solution)/shard_map/all_to_all | solution.py:382
  327.6 10.7 %steps.5 = (f32[2,2,64,256]{3,2,1,0:T(8,128)}, f32[2,2,64,256]{3,2,1,0:T(8,128)}, f32[2,2,64,256]{3,2,1,0:T(8,128)}, f32[2,2,64,256]{3,2,1,0:T(8,128)}) custom-call(s32[1]{0:T(128)} %bitcast.refs_0_, f32[2,2]{1,0:T(2,128)} %bitcast.293, bf16[3,512,1536]{2,1,0:T(8,128)(2,1)} %get-tuple-element.183.refs_2_, bf16[3,1536,512]{2,1,0:T(8,128)(2,1)} %get-tuple-element.184.refs_3_, ...), custom_call_target="tpu_custom_call" | custom-call | tf_op jit(solution)/shard_map/steps/pallas_call | solution.py:250
  338.3 13.9 %steps.6 = (f32[3,2,64,256]{3,2,1,0:T(8,128)}, f32[3,2,64,256]{3,2,1,0:T(8,128)}, f32[3,2,64,256]{3,2,1,0:T(8,128)}, f32[3,2,64,256]{3,2,1,0:T(8,128)}) custom-call(s32[1]{0:T(128)} %bitcast.refs_0_, f32[2,3]{1,0:T(2,128)} %slice.171.refs_1_, bf16[3,512,1536]{2,1,0:T(8,128)(2,1)} %get-tuple-element.183.refs_2_, ...), custom_call_target="tpu_custom_call" | custom-call | tf_op jit(solution)/shard_map/steps/pallas_call | solution.py:250
  352.2 20.4 %steps.7 = (f32[5,2,64,256]{3,2,1,0:T(8,128)}, f32[5,2,64,256]{3,2,1,0:T(8,128)}, f32[5,2,64,256]{3,2,1,0:T(8,128)}, f32[5,2,64,256]{3,2,1,0:T(8,128)}) custom-call(s32[1]{0:T(128)} %bitcast.refs_0_, f32[2,5]{1,0:T(2,128)} %slice.172.refs_1_, bf16[3,512,1536]{2,1,0:T(8,128)(2,1)} %get-tuple-element.183.refs_2_, ...), custom_call_target="tpu_custom_call" | custom-call | tf_op jit(solution)/shard_map/steps/pallas_call | solution.py:250
  372.6 23.6 %steps.8 = (f32[6,2,64,256]{3,2,1,0:T(8,128)}, f32[6,2,64,256]{3,2,1,0:T(8,128)}, f32[6,2,64,256]{3,2,1,0:T(8,128)}, f32[6,2,64,256]{3,2,1,0:T(8,128)}) custom-call(s32[1]{0:T(128)} %bitcast.refs_0_, f32[2,6]{1,0:T(2,128)} %slice.173.refs_1_, bf16[3,512,1536]{2,1,0:T(8,128)(2,1)} %get-tuple-element.183.refs_2_, ...), custom_call_target="tpu_custom_call" | custom-call | tf_op jit(solution)/shard_map/steps/pallas_call | solution.py:250
  409.3 4.5 broadcast_in_dim.2
  417.2 6.8 %collective-permute-done.54 = f32[2,2,64,256]{3,2,1,0:T(8,128)S(1)} collective-permute-done((f32[2,2,64,256]{3,2,1,0:T(8,128)S(1)}, f32[2,2,64,256]{3,2,1,0:T(8,128)S(1)}, u32[]{:S(2)}, u32[]{:S(2)}) %collective-permute-start.54) | collective-permute-done | bytes 262176 | tf_op jit(solution)/shard_map/ppermute | solution.py:72
  424.0 3.5 collective-permute-start.59
  428.3 18.9 %collective-permute-done.55 = f32[2,2,64,256]{3,2,1,0:T(8,128)S(1)} collective-permute-done((f32[2,2,64,256]{3,2,1,0:T(8,128)S(1)}, f32[2,2,64,256]{3,2,1,0:T(8,128)S(1)}, u32[]{:S(2)}, u32[]{:S(2)}) %collective-permute-start.55) | collective-permute-done | bytes 262176 | tf_op jit(solution)/shard_map/ppermute | solution.py:72
  449.4 5.7 collective-permute-done.57
  455.9 37.6 %collective-permute-done.58 = f32[3,2,64,256]{3,2,1,0:T(8,128)S(1)} collective-permute-done((f32[3,2,64,256]{3,2,1,0:T(8,128)S(1)}, f32[3,2,64,256]{3,2,1,0:T(8,128)S(1)}, u32[]{:S(2)}, u32[]{:S(2)}) %collective-permute-start.58) | collective-permute-done | bytes 393248 | tf_op jit(solution)/shard_map/ppermute | solution.py:72
  498.2 7.2 %steps.9 = (f32[1,2,64,256]{3,2,1,0:T(8,128)}, f32[1,2,64,256]{3,2,1,0:T(8,128)}, f32[1,2,64,256]{3,2,1,0:T(8,128)}, f32[1,2,64,256]{3,2,1,0:T(8,128)}) custom-call(s32[1]{0:T(128)} %bitcast.refs_0_, f32[2,1]{1,0:T(2,128)} %copy.25.refs_1_, bf16[3,512,1536]{2,1,0:T(8,128)(2,1)} %get-tuple-element.183.refs_2_, ...), custom_call_target="tpu_custom_call" | custom-call | tf_op jit(solution)/shard_map/steps/pallas_call | solution.py:250
  511.7 43.7 %collective-permute-done.61 = f32[5,2,64,256]{3,2,1,0:T(8,128)S(1)} collective-permute-done((f32[5,2,64,256]{3,2,1,0:T(8,128)}, f32[5,2,64,256]{3,2,1,0:T(8,128)S(1)}, u32[]{:S(2)}, u32[]{:S(2)}) %collective-permute-start.61) | collective-permute-done | bytes 655392 | tf_op jit(solution)/shard_map/ppermute | solution.py:72
  558.2 12.2 %collective-permute-done.63 = f32[6,2,64,256]{3,2,1,0:T(8,128)S(1)} collective-permute-done((f32[6,2,64,256]{3,2,1,0:T(8,128)}, f32[6,2,64,256]{3,2,1,0:T(8,128)S(1)}, u32[]{:S(2)}, u32[]{:S(2)}) %collective-permute-start.63) | collective-permute-done | bytes 786464 | tf_op jit(solution)/shard_map/ppermute | solution.py:72
  571.4 16.1 %collective-permute-done.64 = f32[6,2,64,256]{3,2,1,0:T(8,128)S(1)} collective-permute-done((f32[6,2,64,256]{3,2,1,0:T(8,128)}, f32[6,2,64,256]{3,2,1,0:T(8,128)S(1)}, u32[]{:S(2)}, u32[]{:S(2)}) %collective-permute-start.64) | collective-permute-done | bytes 786464 | tf_op jit(solution)/shard_map/ppermute | solution.py:72
  (323 shorter events, 119.8 us)
Async XLA Ops:
  14.2 20.7 %collective-permute-start.10 = (f32[512,128]{1,0:T(8,128)}, f32[512,128]{1,0:T(8,128)S(1)}, u32[]{:S(2)}, u32[]{:S(2)}) collective-permute-start(f32[512,128]{1,0:T(8,128)} %bitcast.314), channel_id=1, source_target_pairs={{0,16},{4,20},{8,24},{12,28},{16,0},{20,4},{24,8},{28,12},{1,17},{... | collective-permute-start | bytes 786440 | tf_op jit(solution)/shard_map/ppermute | solution.py:72
  15.8 23.7 %collective-permute-start.11 = (f32[512,128]{1,0:T(8,128)}, f32[512,128]{1,0:T(8,128)S(1)}, u32[]{:S(2)}, u32[]{:S(2)}) collective-permute-start(f32[512,128]{1,0:T(8,128)} %bitcast.313), channel_id=1, source_target_pairs={{0,20},{4,16},{8,28},{12,24},{16,4},{20,0},{24,12},{28,8},{1,21},{... | collective-permute-start | bytes 786440 | tf_op jit(solution)/shard_map/ppermute | solution.py:72
  16.1 26.7 %collective-permute-start.12 = (f32[512,128]{1,0:T(8,128)}, f32[512,128]{1,0:T(8,128)S(1)}, u32[]{:S(2)}, u32[]{:S(2)}) collective-permute-start(f32[512,128]{1,0:T(8,128)} %bitcast.312), channel_id=1, source_target_pairs={{0,24},{4,28},{8,16},{12,20},{16,8},{20,12},{24,0},{28,4},{1,25},{... | collective-permute-start | bytes 786440 | tf_op jit(solution)/shard_map/ppermute | solution.py:72
  17.6 25.2 %collective-permute-start.13 = (f32[512,128]{1,0:T(8,128)}, f32[512,128]{1,0:T(8,128)S(1)}, u32[]{:S(2)}, u32[]{:S(2)}) collective-permute-start(f32[512,128]{1,0:T(8,128)} %bitcast.311), channel_id=1, source_target_pairs={{0,28},{4,24},{8,20},{12,16},{16,12},{20,8},{24,4},{28,0},{1,29},{... | collective-permute-start | bytes 786440 | tf_op jit(solution)/shard_map/ppermute | solution.py:72
  18.7 24.1 %collective-permute-start.7 = (f32[512,128]{1,0:T(8,128)}, f32[512,128]{1,0:T(8,128)S(1)}, u32[]{:S(2)}, u32[]{:S(2)}) collective-permute-start(f32[512,128]{1,0:T(8,128)} %bitcast.310), channel_id=1, source_target_pairs={{0,4},{4,0},{8,12},{12,8},{16,20},{20,16},{24,28},{28,24},{1,5},{5... | collective-permute-start | bytes 786440 | tf_op jit(solution)/shard_map/ppermute | solution.py:72
  53.6 59.7 %all-to-all-start = ((f32[32,128,128]{2,1,0:T(8,128)}), f32[32,128,128]{2,1,0:T(8,128)S(1)}, u32[]{:S(2)}, u32[]{:S(2)}) async-start(f32[32,128,128]{2,1,0:T(8,128)} %bitcast.248), calls=%async_computation | async-start | bytes 4194304 | tf_op jit(solution)/shard_map/all_to_all | solution.py:382
  61.5 19.8 %collective-permute-start.16 = (f32[512,128]{1,0:T(8,128)}, f32[512,128]{1,0:T(8,128)S(1)}, u32[]{:S(2)}, u32[]{:S(2)}) collective-permute-start(f32[512,128]{1,0:T(8,128)} %bitcast.325), channel_id=1, source_target_pairs={{0,8},{4,12},{8,0},{12,4},{16,24},{20,28},{24,16},{28,20},{1,9},{5... | collective-permute-start | bytes 786440 | tf_op jit(solution)/shard_map/ppermute | solution.py:72
  63.0 25.9 %collective-permute-start.17 = (f32[512,128]{1,0:T(8,128)}, f32[512,128]{1,0:T(8,128)S(1)}, u32[]{:S(2)}, u32[]{:S(2)}) collective-permute-start(f32[512,128]{1,0:T(8,128)} %bitcast.323), channel_id=1, source_target_pairs={{0,12},{4,8},{8,4},{12,0},{16,28},{20,24},{24,20},{28,16},{1,13},{... | collective-permute-start | bytes 786440 | tf_op jit(solution)/shard_map/ppermute | solution.py:72
  63.2 25.6 %collective-permute-start.18 = (f32[512,128]{1,0:T(8,128)}, f32[512,128]{1,0:T(8,128)S(1)}, u32[]{:S(2)}, u32[]{:S(2)}) collective-permute-start(f32[512,128]{1,0:T(8,128)} %bitcast.321), channel_id=1, source_target_pairs={{0,16},{4,20},{8,24},{12,28},{16,0},{20,4},{24,8},{28,12},{1,17},{... | collective-permute-start | bytes 786440 | tf_op jit(solution)/shard_map/ppermute | solution.py:72
  64.7 27.4 %collective-permute-start.19 = (f32[512,128]{1,0:T(8,128)}, f32[512,128]{1,0:T(8,128)S(1)}, u32[]{:S(2)}, u32[]{:S(2)}) collective-permute-start(f32[512,128]{1,0:T(8,128)} %bitcast.319), channel_id=1, source_target_pairs={{0,20},{4,16},{8,28},{12,24},{16,4},{20,0},{24,12},{28,8},{1,21},{... | collective-permute-start | bytes 786440 | tf_op jit(solution)/shard_map/ppermute | solution.py:72
  65.0 35.6 %collective-permute-start.20 = (f32[512,128]{1,0:T(8,128)}, f32[512,128]{1,0:T(8,128)}, u32[]{:S(2)}, u32[]{:S(2)}) collective-permute-start(f32[512,128]{1,0:T(8,128)} %bitcast.317), channel_id=1, source_target_pairs={{0,24},{4,28},{8,16},{12,20},{16,8},{20,12},{24,0},{28,4},{1,25},{... | collective-permute-start | bytes 786440 | tf_op jit(solution)/shard_map/ppermute | solution.py:72
  81.3 26.2 %collective-permute-start.21 = (f32[512,128]{1,0:T(8,128)}, f32[512,128]{1,0:T(8,128)}, u32[]{:S(2)}, u32[]{:S(2)}) collective-permute-start(f32[512,128]{1,0:T(8,128)} %bitcast.315), channel_id=1, source_target_pairs={{0,28},{4,24},{8,20},{12,16},{16,12},{20,8},{24,4},{28,0},{1,29},{... | collective-permute-start | bytes 786440 | tf_op jit(solution)/shard_map/ppermute | solution.py:72
  114.6 59.6 %all-to-all-start.1 = ((f32[32,128,128]{2,1,0:T(8,128)}), f32[32,128,128]{2,1,0:T(8,128)}, u32[]{:S(2)}, u32[]{:S(2)}) async-start(f32[32,128,128]{2,1,0:T(8,128)} %bitcast.247), calls=%async_computation.1 | async-start | bytes 4194304 | tf_op jit(solution)/shard_map/all_to_all | solution.py:382
  121.9 19.8 %collective-permute-start.40 = (f32[512,128]{1,0:T(8,128)}, f32[512,128]{1,0:T(8,128)S(1)}, u32[]{:S(2)}, u32[]{:S(2)}) collective-permute-start(f32[512,128]{1,0:T(8,128)} %bitcast.326), channel_id=1, source_target_pairs={{0,8},{4,12},{8,0},{12,4},{16,24},{20,28},{24,16},{28,20},{1,9},{5... | collective-permute-start | bytes 786440 | tf_op jit(solution)/shard_map/ppermute | solution.py:72
  123.4 25.9 %collective-permute-start.41 = (f32[512,128]{1,0:T(8,128)}, f32[512,128]{1,0:T(8,128)S(1)}, u32[]{:S(2)}, u32[]{:S(2)}) collective-permute-start(f32[512,128]{1,0:T(8,128)} %bitcast.324), channel_id=1, source_target_pairs={{0,12},{4,8},{8,4},{12,0},{16,28},{20,24},{24,20},{28,16},{1,13},{... | collective-permute-start | bytes 786440 | tf_op jit(solution)/shard_map/ppermute | solution.py:72
  123.6 25.6 %collective-permute-start.42 = (f32[512,128]{1,0:T(8,128)}, f32[512,128]{1,0:T(8,128)S(1)}, u32[]{:S(2)}, u32[]{:S(2)}) collective-permute-start(f32[512,128]{1,0:T(8,128)} %bitcast.322), channel_id=1, source_target_pairs={{0,16},{4,20},{8,24},{12,28},{16,0},{20,4},{24,8},{28,12},{1,17},{... | collective-permute-start | bytes 786440 | tf_op jit(solution)/shard_map/ppermute | solution.py:72
  125.1 27.4 %collective-permute-start.43 = (f32[512,128]{1,0:T(8,128)}, f32[512,128]{1,0:T(8,128)S(1)}, u32[]{:S(2)}, u32[]{:S(2)}) collective-permute-start(f32[512,128]{1,0:T(8,128)} %bitcast.320), channel_id=1, source_target_pairs={{0,20},{4,16},{8,28},{12,24},{16,4},{20,0},{24,12},{28,8},{1,21},{... | collective-permute-start | bytes 786440 | tf_op jit(solution)/shard_map/ppermute | solution.py:72
  125.4 35.5 %collective-permute-start.44 = (f32[512,128]{1,0:T(8,128)}, f32[512,128]{1,0:T(8,128)S(1)}, u32[]{:S(2)}, u32[]{:S(2)}) collective-permute-start(f32[512,128]{1,0:T(8,128)} %bitcast.318), channel_id=1, source_target_pairs={{0,24},{4,28},{8,16},{12,20},{16,8},{20,12},{24,0},{28,4},{1,25},{... | collective-permute-start | bytes 786440 | tf_op jit(solution)/shard_map/ppermute | solution.py:72
  141.7 26.1 %collective-permute-start.45 = (f32[512,128]{1,0:T(8,128)}, f32[512,128]{1,0:T(8,128)S(1)}, u32[]{:S(2)}, u32[]{:S(2)}) collective-permute-start(f32[512,128]{1,0:T(8,128)} %bitcast.316), channel_id=1, source_target_pairs={{0,28},{4,24},{8,20},{12,16},{16,12},{20,8},{24,4},{28,0},{1,29},{... | collective-permute-start | bytes 786440 | tf_op jit(solution)/shard_map/ppermute | solution.py:72
  174.2 100.3 %all-to-all-start.2 = ((f32[32,128,128]{2,1,0:T(8,128)}), f32[32,128,128]{2,1,0:T(8,128)S(1)}, u32[]{:S(2)}, u32[]{:S(2)}) async-start(f32[32,128,128]{2,1,0:T(8,128)} %bitcast.245), calls=%async_computation.2 | async-start | bytes 4194304 | tf_op jit(solution)/shard_map/all_to_all | solution.py:382
  196.4 22.1 %collective-permute-start.4 = (f32[2,2,32,256]{3,2,1,0:T(8,128)S(1)}, f32[2,2,32,256]{3,2,1,0:T(8,128)S(1)}, u32[]{:S(2)}, u32[]{:S(2)}) collective-permute-start(f32[2,2,32,256]{3,2,1,0:T(8,128)S(1)} %fusion.4), channel_id=1, source_target_pairs={{0,1},{1,0},{2,3},{3,2},{4,5},{5,4},{6,7},{7,6},{8,9},{9,8},{10,11... | collective-permute-start | bytes 393224 | tf_op jit(solution)/shard_map/ppermute | solution.py:72
  202.4 31.8 %collective-permute-start.5 = (f32[2,2,32,256]{3,2,1,0:T(8,128)S(1)}, f32[2,2,32,256]{3,2,1,0:T(8,128)S(1)}, u32[]{:S(2)}, u32[]{:S(2)}) collective-permute-start(f32[2,2,32,256]{3,2,1,0:T(8,128)S(1)} %fusion.4), channel_id=1, source_target_pairs={{0,2},{1,3},{2,0},{3,1},{4,6},{5,7},{6,4},{7,5},{8,10},{9,11},{10,... | collective-permute-start | bytes 393224 | tf_op jit(solution)/shard_map/ppermute | solution.py:72
  202.4 35.3 %collective-permute-start.6 = (f32[2,2,32,256]{3,2,1,0:T(8,128)S(1)}, f32[2,2,32,256]{3,2,1,0:T(8,128)S(1)}, u32[]{:S(2)}, u32[]{:S(2)}) collective-permute-start(f32[2,2,32,256]{3,2,1,0:T(8,128)S(1)} %fusion.4), channel_id=1, source_target_pairs={{0,3},{1,2},{2,1},{3,0},{4,7},{5,6},{6,5},{7,4},{8,11},{9,10},{10,... | collective-permute-start | bytes 393224 | tf_op jit(solution)/shard_map/ppermute | solution.py:72
  204.0 35.6 %collective-permute-start.29 = (f32[2,8,256]{2,1,0:T(8,128)S(1)}, f32[2,8,256]{2,1,0:T(8,128)S(1)}, u32[]{:S(2)}, u32[]{:S(2)}) collective-permute-start(f32[2,8,256]{2,1,0:T(8,128)S(1)} %add_add_fusion), channel_id=1, source_target_pairs={{0,1},{1,0},{2,3},{3,2},{4,5},{5,4},{6,7},{7,6},{8,9},{9,8},{10,11... | collective-permute-start | bytes 49160 | tf_op jit(solution)/shard_map/ppermute | solution.py:72
  206.9 33.5 %collective-permute-start.30 = (f32[2,8,256]{2,1,0:T(8,128)S(1)}, f32[2,8,256]{2,1,0:T(8,128)S(1)}, u32[]{:S(2)}, u32[]{:S(2)}) collective-permute-start(f32[2,8,256]{2,1,0:T(8,128)S(1)} %add_add_fusion), channel_id=1, source_target_pairs={{0,2},{1,3},{2,0},{3,1},{4,6},{5,7},{6,4},{7,5},{8,10},{9,11},{10,... | collective-permute-start | bytes 49160 | tf_op jit(solution)/shard_map/ppermute | solution.py:72
  218.5 23.4 %collective-permute-start.31 = (f32[2,8,256]{2,1,0:T(8,128)S(1)}, f32[2,8,256]{2,1,0:T(8,128)S(1)}, u32[]{:S(2)}, u32[]{:S(2)}) collective-permute-start(f32[2,8,256]{2,1,0:T(8,128)S(1)} %add_add_fusion), channel_id=1, source_target_pairs={{0,3},{1,2},{2,1},{3,0},{4,7},{5,6},{6,5},{7,4},{8,11},{9,10},{10,... | collective-permute-start | bytes 49160 | tf_op jit(solution)/shard_map/ppermute | solution.py:72
  241.9 38.1 %collective-permute-start.14 = (f32[4,2,2,32,256]{4,3,2,1,0:T(8,128)S(1)}, f32[4,2,2,32,256]{4,3,2,1,0:T(8,128)S(1)}, u32[]{:S(2)}, u32[]{:S(2)}) collective-permute-start(f32[4,2,2,32,256]{4,3,2,1,0:T(8,128)S(1)} %fusion.3), channel_id=1, source_target_pairs={{0,4},{4,0},{8,12},{12,8},{16,20},{20,16},{24,28},{28,24},{1,5},{5... | collective-permute-start | bytes 1572872 | tf_op jit(solution)/shard_map/ppermute | solution.py:72
  242.3 23.4 %collective-permute-start.50 = (f32[512,128]{1,0:T(8,128)S(1)}, f32[512,128]{1,0:T(8,128)S(1)}, u32[]{:S(2)}, u32[]{:S(2)}) collective-permute-start(f32[512,128]{1,0:T(8,128)S(1)} %bitcast.304), channel_id=1, source_target_pairs={{0,20},{4,16},{8,28},{12,24},{16,4},{20,0},{24,12},{28,8},{1,21},{... | collective-permute-start | bytes 786440 | tf_op jit(solution)/shard_map/ppermute | solution.py:72
  247.1 20.0 %collective-permute-start.51 = (f32[512,128]{1,0:T(8,128)S(1)}, f32[512,128]{1,0:T(8,128)S(1)}, u32[]{:S(2)}, u32[]{:S(2)}) collective-permute-start(f32[512,128]{1,0:T(8,128)S(1)} %bitcast.303), channel_id=1, source_target_pairs={{0,24},{4,28},{8,16},{12,20},{16,8},{20,12},{24,0},{28,4},{1,25},{... | collective-permute-start | bytes 786440 | tf_op jit(solution)/shard_map/ppermute | solution.py:72
  254.8 26.6 %collective-permute-start.32 = (f32[4,2,8,256]{3,2,0,1:T(8,128)S(1)}, f32[4,2,8,256]{3,2,0,1:T(8,128)S(1)}, u32[]{:S(2)}, u32[]{:S(2)}) collective-permute-start(f32[4,2,8,256]{3,2,0,1:T(8,128)S(1)} %select_select_fusion.3), channel_id=1, source_target_pairs={{0,4},{4,0},{8,12},{12,8},{16,20},{20,16},{24,28},{28,24},{1,5},{5... | collective-permute-start | bytes 196616 | tf_op jit(solution)/shard_map/ppermute | solution.py:72
  267.1 18.3 %collective-permute-start.34 = (f32[4,2,8,256]{3,2,0,1:T(8,128)S(1)}, f32[4,2,8,256]{3,2,0,1:T(8,128)}, u32[]{:S(2)}, u32[]{:S(2)}) collective-permute-start(f32[4,2,8,256]{3,2,0,1:T(8,128)S(1)} %select_select_fusion.3), channel_id=1, source_target_pairs={{0,12},{4,8},{8,4},{12,0},{16,28},{20,24},{24,20},{28,16},{1,13},{... | collective-permute-start | bytes 196616 | tf_op jit(solution)/shard_map/ppermute | solution.py:72
  267.3 19.6 %collective-permute-start.35 = (f32[4,2,8,256]{3,2,0,1:T(8,128)S(1)}, f32[4,2,8,256]{3,2,0,1:T(8,128)}, u32[]{:S(2)}, u32[]{:S(2)}) collective-permute-start(f32[4,2,8,256]{3,2,0,1:T(8,128)S(1)} %select_select_fusion.3), channel_id=1, source_target_pairs={{0,16},{4,20},{8,24},{12,28},{16,0},{20,4},{24,8},{28,12},{1,17},{... | collective-permute-start | bytes 196616 | tf_op jit(solution)/shard_map/ppermute | solution.py:72
  275.8 51.8 %all-to-all-start.3 = ((f32[32,128,128]{2,1,0:T(8,128)}), f32[32,128,128]{2,1,0:T(8,128)}, u32[]{:S(2)}, u32[]{:S(2)}) async-start(f32[32,128,128]{2,1,0:T(8,128)} %bitcast.246), calls=%async_computation.3 | async-start | bytes 4194304 | tf_op jit(solution)/shard_map/all_to_all | solution.py:382
  285.3 110.9 %collective-permute-start.65 = (f32[4,8,128]{2,1,0:T(8,128)S(1)}, f32[4,8,128]{2,1,0:T(8,128)S(1)}, u32[]{:S(2)}, u32[]{:S(2)}) collective-permute-start(f32[4,8,128]{2,1,0:T(8,128)S(1)} %pad_maximum_fusion.19), channel_id=1, source_target_pairs={{0,1},{1,0},{2,3},{3,2},{4,5},{5,4},{6,7},{7,6},{8,9},{9,8},{10,11... | collective-permute-start | bytes 49160 | tf_op jit(solution)/shard_map/ppermute | solution.py:72
  286.9 109.4 %collective-permute-start.66 = (f32[4,8,128]{2,1,0:T(8,128)S(1)}, f32[4,8,128]{2,1,0:T(8,128)S(1)}, u32[]{:S(2)}, u32[]{:S(2)}) collective-permute-start(f32[4,8,128]{2,1,0:T(8,128)S(1)} %pad_maximum_fusion.19), channel_id=1, source_target_pairs={{0,2},{1,3},{2,0},{3,1},{4,6},{5,7},{6,4},{7,5},{8,10},{9,11},{10,... | collective-permute-start | bytes 49160 | tf_op jit(solution)/shard_map/ppermute | solution.py:72
  295.4 100.9 %collective-permute-start.67 = (f32[4,8,128]{2,1,0:T(8,128)S(1)}, f32[4,8,128]{2,1,0:T(8,128)S(1)}, u32[]{:S(2)}, u32[]{:S(2)}) collective-permute-start(f32[4,8,128]{2,1,0:T(8,128)S(1)} %pad_maximum_fusion.19), channel_id=1, source_target_pairs={{0,3},{1,2},{2,1},{3,0},{4,7},{5,6},{6,5},{7,4},{8,11},{9,10},{10,... | collective-permute-start | bytes 49160 | tf_op jit(solution)/shard_map/ppermute | solution.py:72
  404.9 19.1 %collective-permute-start.54 = (f32[2,2,64,256]{3,2,1,0:T(8,128)S(1)}, f32[2,2,64,256]{3,2,1,0:T(8,128)S(1)}, u32[]{:S(2)}, u32[]{:S(2)}) collective-permute-start(f32[2,2,64,256]{3,2,1,0:T(8,128)S(1)} %copy-done.50), channel_id=1, source_target_pairs={{0,2},{1,3},{2,0},{3,1},{4,6},{5,7},{6,4},{7,5},{8,10},{9,11},{10,... | collective-permute-start | bytes 786440 | tf_op jit(solution)/shard_map/ppermute | solution.py:72
  406.2 40.9 %collective-permute-start.55 = (f32[2,2,64,256]{3,2,1,0:T(8,128)S(1)}, f32[2,2,64,256]{3,2,1,0:T(8,128)S(1)}, u32[]{:S(2)}, u32[]{:S(2)}) collective-permute-start(f32[2,2,64,256]{3,2,1,0:T(8,128)S(1)} %copy-done.49), channel_id=1, source_target_pairs={{0,3},{1,2},{2,1},{3,0},{4,7},{5,6},{6,5},{7,4},{8,11},{9,10},{10,... | collective-permute-start | bytes 786440 | tf_op jit(solution)/shard_map/ppermute | solution.py:72
  407.7 41.0 %collective-permute-start.56 = (f32[3,2,64,256]{3,2,1,0:T(8,128)S(1)}, f32[3,2,64,256]{3,2,1,0:T(8,128)S(1)}, u32[]{:S(2)}, u32[]{:S(2)}) collective-permute-start(f32[3,2,64,256]{3,2,1,0:T(8,128)S(1)} %copy-done.43), channel_id=1, source_target_pairs={{0,1},{1,0},{2,3},{3,2},{4,5},{5,4},{6,7},{7,6},{8,9},{9,8},{10,11... | collective-permute-start | bytes 1179656 | tf_op jit(solution)/shard_map/ppermute | solution.py:72
  414.5 40.6 %collective-permute-start.57 = (f32[3,2,64,256]{3,2,1,0:T(8,128)S(1)}, f32[3,2,64,256]{3,2,1,0:T(8,128)S(1)}, u32[]{:S(2)}, u32[]{:S(2)}) collective-permute-start(f32[3,2,64,256]{3,2,1,0:T(8,128)S(1)} %copy-done.42), channel_id=1, source_target_pairs={{0,2},{1,3},{2,0},{3,1},{4,6},{5,7},{6,4},{7,5},{8,10},{9,11},{10,... | collective-permute-start | bytes 1179656 | tf_op jit(solution)/shard_map/ppermute | solution.py:72
  416.1 77.4 %collective-permute-start.58 = (f32[3,2,64,256]{3,2,1,0:T(8,128)S(1)}, f32[3,2,64,256]{3,2,1,0:T(8,128)S(1)}, u32[]{:S(2)}, u32[]{:S(2)}) collective-permute-start(f32[3,2,64,256]{3,2,1,0:T(8,128)S(1)} %copy-done.41), channel_id=1, source_target_pairs={{0,3},{1,2},{2,1},{3,0},{4,7},{5,6},{6,5},{7,4},{8,11},{9,10},{10,... | collective-permute-start | bytes 1179656 | tf_op jit(solution)/shard_map/ppermute | solution.py:72
  424.0 81.4 %collective-permute-start.59 = (f32[5,2,64,256]{3,2,1,0:T(8,128)}, f32[5,2,64,256]{3,2,1,0:T(8,128)S(1)}, u32[]{:S(2)}, u32[]{:S(2)}) collective-permute-start(f32[5,2,64,256]{3,2,1,0:T(8,128)} %get-tuple-element.207), channel_id=1, source_target_pairs={{0,1},{1,0},{2,3},{3,2},{4,5},{5,4},{6,7},{7,6},{8,9},{9,8},{10,11... | collective-permute-start | bytes 1966088 | tf_op jit(solution)/shard_map/ppermute | solution.py:72
  447.2 63.7 %collective-permute-start.60 = (f32[5,2,64,256]{3,2,1,0:T(8,128)}, f32[5,2,64,256]{3,2,1,0:T(8,128)S(1)}, u32[]{:S(2)}, u32[]{:S(2)}) collective-permute-start(f32[5,2,64,256]{3,2,1,0:T(8,128)} %get-tuple-element.208), channel_id=1, source_target_pairs={{0,2},{1,3},{2,0},{3,1},{4,6},{5,7},{6,4},{7,5},{8,10},{9,11},{10,... | collective-permute-start | bytes 1966088 | tf_op jit(solution)/shard_map/ppermute | solution.py:72
  448.7 106.7 %collective-permute-start.61 = (f32[5,2,64,256]{3,2,1,0:T(8,128)}, f32[5,2,64,256]{3,2,1,0:T(8,128)S(1)}, u32[]{:S(2)}, u32[]{:S(2)}) collective-permute-start(f32[5,2,64,256]{3,2,1,0:T(8,128)} %get-tuple-element.209), channel_id=1, source_target_pairs={{0,3},{1,2},{2,1},{3,0},{4,7},{5,6},{6,5},{7,4},{8,11},{9,10},{10,... | collective-permute-start | bytes 1966088 | tf_op jit(solution)/shard_map/ppermute | solution.py:72
  455.1 40.1 %collective-permute-start.70 = (f32[2,2,4,4,8,128]{5,4,3,2,0,1:T(8,128)S(1)}, f32[2,2,4,4,8,128]{5,4,3,2,0,1:T(8,128)S(1)}, u32[]{:S(2)}, u32[]{:S(2)}) collective-permute-start(f32[2,2,4,4,8,128]{5,4,3,2,0,1:T(8,128)S(1)} %pad_maximum_fusion.11), channel_id=1, source_target_pairs={{0,4},{4,0},{8,12},{12,8},{16,20},{20,16},{24,28},{28,24},{1,5},{5... | collective-permute-start | bytes 786440 | tf_op jit(solution)/shard_map/ppermute | solution.py:72
  493.5 63.7 %collective-permute-start.62 = (f32[6,2,64,256]{3,2,1,0:T(8,128)}, f32[6,2,64,256]{3,2,1,0:T(8,128)S(1)}, u32[]{:S(2)}, u32[]{:S(2)}) collective-permute-start(f32[6,2,64,256]{3,2,1,0:T(8,128)} %get-tuple-element.212), channel_id=1, source_target_pairs={{0,1},{1,0},{2,3},{3,2},{4,5},{5,4},{6,7},{7,6},{8,9},{9,8},{10,11... | collective-permute-start | bytes 2359304 | tf_op jit(solution)/shard_map/ppermute | solution.py:72
  495.2 75.2 %collective-permute-start.63 = (f32[6,2,64,256]{3,2,1,0:T(8,128)}, f32[6,2,64,256]{3,2,1,0:T(8,128)S(1)}, u32[]{:S(2)}, u32[]{:S(2)}) collective-permute-start(f32[6,2,64,256]{3,2,1,0:T(8,128)} %get-tuple-element.213), channel_id=1, source_target_pairs={{0,2},{1,3},{2,0},{3,1},{4,6},{5,7},{6,4},{7,5},{8,10},{9,11},{10,... | collective-permute-start | bytes 2359304 | tf_op jit(solution)/shard_map/ppermute | solution.py:72
  505.4 82.1 %collective-permute-start.64 = (f32[6,2,64,256]{3,2,1,0:T(8,128)}, f32[6,2,64,256]{3,2,1,0:T(8,128)S(1)}, u32[]{:S(2)}, u32[]{:S(2)}) collective-permute-start(f32[6,2,64,256]{3,2,1,0:T(8,128)} %get-tuple-element.214), channel_id=1, source_target_pairs={{0,3},{1,2},{2,1},{3,0},{4,7},{5,6},{6,5},{7,4},{8,11},{9,10},{10,... | collective-permute-start | bytes 2359304 | tf_op jit(solution)/shard_map/ppermute | solution.py:72
  (80 other events, 928.4 us)
